TPU v7x, 1024 devices: a whole 8x8x8 slice. The times are simulated.
1024 devices in a mesh: grp: 8 (over x_hi, core), row: 8 (over y), col: 16 (over x_lo, z).
Axes of the slice: x: 8 (x_hi: 4, x_lo: 2; x = x_hi * 2 + x_lo), y: 8, z: 8, core: 2. Of those that a mesh axis runs over, the one named last changes fastest.
Arguments:
- amplitudes: bfloat16 [64, 16, 256, 256], P(('grp', 'row'), 'col'), may hold values from -6 to 6
- factors: bfloat16 [16, 256, 256], P('col'), may hold values from -0.1875 to 0.1875
- cycle_weight: bfloat16 [16384, 16384], P('col', 'row'), may hold values from -0.046875 to 0.046875
- orbital_order: int32 [256], replicated, may hold values from 0 to 255, each once
Outputs:
- ladder_term: bfloat16 [64, 16, 256, 256], P(('grp', 'row'), 'col')
- cycle_term: bfloat16 [4096, 16384], P(('grp', 'row'), 'col')
Inputs may be any that keep to these rules, and one draw needn't show every extreme that they name: `orbital_order`: each of 0 to 255 appears exactly once.
All inputs are finite; a program needn't handle non-finite values.
Results may differ from a plain program's by a relative error of at most 0.0049.
Values may be sent and summed in bfloat16 or wider, within the bound.
No kernel may reach another device: no remote copies, remote signals or barrier semaphores. Data moves between devices by JAX's collectives and lax.ppermute only.
A program may use at most 64 MiB of HBM per device.

v0:
```python
import jax
import jax.numpy as jnp
from jax import lax
from jax.experimental import pallas as pl
from jax.experimental.pallas import tpu as pltpu
from jax.sharding import Mesh, PartitionSpec as P

AXES = ("hi", "core", "rowpair", "side", "lo", "z")


SHIFTS = (3, -3, 2, -2, 1, -1, 4)


def shift(x, by):
    depth = lax.axis_size("z")
    return lax.ppermute(x, "z", [(i, (i + by) % depth) for i in range(depth)])


def swap(x, axis):
    return lax.ppermute(x, axis, [(0, 1), (1, 0)])


def tied(x, *after):
    return lax.optimization_barrier((x, *after))[0]


def exchange(x, axes):
    return lax.all_to_all(x, axes, 0, 0, tiled=True)


def in_order(mine, other, axis, dim):
    first = lax.axis_index(axis) == 0
    return jnp.concatenate([jnp.where(first, mine, other), jnp.where(first, other, mine)], axis=dim)


def join_kernel(*refs):
    pieces, out_ref = refs[:-1], refs[-1]
    count = pieces[0].shape[0]
    for i, piece in enumerate(pieces):
        out_ref[pl.ds(i * count, count)] = piece[...]


def joined(blocks):
    shape = (len(blocks) * blocks[0].shape[0], *blocks[0].shape[1:])
    size = 4 * blocks[0].size * len(blocks)
    return pl.pallas_call(
        join_kernel,
        in_specs=[pl.BlockSpec(memory_space=pltpu.VMEM)] * len(blocks),
        out_specs=pl.BlockSpec(memory_space=pltpu.VMEM),
        out_shape=jax.ShapeDtypeStruct(shape, blocks[0].dtype),
        cost_estimate=pl.CostEstimate(flops=0, bytes_accessed=size, transcendentals=0),
        name="join",
    )(*blocks)


def product(panel, weight):
    return lax.dot_general(panel, weight, (((1,), (1,)), ((), ())), preferred_element_type=jnp.float32)


def sums_of(panel, weights):
    panel = panel.reshape(-1, panel.shape[-1])
    inner = panel.shape[1] // 2
    here, there = panel[:, :inner], panel[:, inner:]
    return jnp.concatenate(
        [(product(here, a) + product(there, b)).astype(jnp.bfloat16) for a, b in weights], axis=1
    )


def body(amplitudes, factors, cycle_weight, orbital_order):
    virtual = amplitudes.shape[2]
    pair = amplitudes.reshape(virtual, virtual)
    groups = lax.axis_size("hi") * lax.axis_size("core")
    pairs = lax.axis_size("rowpair")
    depth = lax.axis_size("z")
    occupied = groups * pairs * 2
    width = virtual // groups // 2
    block = virtual // pairs
    outs, inner = cycle_weight.shape
    core = lax.axis_index("core")

    half = virtual // 2
    mine = lax.dynamic_slice_in_dim(factors, core * half, half, axis=1)
    both = jnp.concatenate([mine, swap(mine, "lo")])

    pick = (orbital_order[:, None] == jnp.arange(virtual, dtype=jnp.int32)[None, :]).astype(jnp.bfloat16)
    ordered = jnp.einsum("xd,cd->xc", pick, pair, preferred_element_type=jnp.float32).astype(jnp.bfloat16)
    tiles = ordered.reshape(groups, 2, width, pairs, block)
    tiles = jnp.transpose(tiles, (0, 3, 1, 2, 4)).reshape(occupied, width * block // 128, 128)
    arrived = exchange(tiles, ("hi", "core", "rowpair", "side"))

    part = outs // 2
    near_weight = lax.dynamic_slice_in_dim(cycle_weight, core * part, part, axis=0)
    last_weight = lax.dynamic_slice_in_dim(cycle_weight, (1 - core) * part, part, axis=0)
    near_other = swap(near_weight, "side")
    last_other = swap(near_other, "core")

    own = arrived.reshape(occupied, width, 2, block // 2)
    own = jnp.transpose(own, (2, 1, 3, 0)).reshape(2, width, inner)
    first = lax.axis_index("side") == 0
    own = jnp.concatenate([jnp.where(first, own[0], own[1]), jnp.where(first, own[1], own[0])], axis=1)

    copies = jnp.broadcast_to(own, (depth, *own.shape))
    near = exchange(copies, "z")
    blocks = [both] + [shift(both, by) for by in SHIFTS]

    far = swap(near, "lo")
    weights = ((near_weight, near_other), (last_weight, last_other))
    near_sums = sums_of(near, weights)
    far_sums = sums_of(tied(far, near_sums), weights)
    parts = in_order(near_sums.reshape(pairs, -1, outs), far_sums.reshape(pairs, -1, outs), "lo", 0)
    parts = exchange(parts, ("rowpair", "side"))
    halves = joined(blocks)
    others = swap(halves, "core")
    whole = jnp.concatenate([halves, others], axis=1)
    dressed = jnp.einsum("pac,cd->pad", whole, pair, preferred_element_type=jnp.float32).astype(jnp.bfloat16)
    ladder = jnp.einsum("pad,pbd->ab", dressed, whole, preferred_element_type=jnp.float32)
    swapped = jnp.roll(ladder, (half, half), (0, 1))
    ladder_term = jnp.where(core == 0, ladder, swapped).astype(jnp.bfloat16).reshape(amplitudes.shape)
    parts = tied(parts, ladder_term)
    total = jnp.sum(parts.reshape(pairs, 2, 2, width, outs).astype(jnp.float32), axis=0)
    total = jnp.transpose(total, (1, 0, 2, 3)).reshape(4 * width, outs).astype(jnp.bfloat16)
    cycle_term = in_order(total[:, :part], total[:, part:], "core", 1)

    return (ladder_term, cycle_term)


def solution(mesh):
    groups, rows, cols = mesh.devices.shape
    split = Mesh(mesh.devices.reshape(groups // 2, 2, rows // 2, 2, 2, cols // 2), AXES)
    row, col = ("rowpair", "side"), ("lo", "z")
    pairs = P(("hi", "core", *row), col, None, None)
    return jax.shard_map(
        body,
        mesh=split,
        in_specs=(pairs, P(col, None, None), P(col, row), P()),
        out_specs=(pairs, P(("hi", "core", *row), col)),
        check_vma=False,
    )
```

profile of v0, /device:TPU:1, one launch (start us, length us, event | category | flops | bytes accessed | tf_op | source)
XLA Modules:
  0.0 170.2 jit_solution(301967525852332535)
XLA Ops:
  1.5 0.9 convolution_convert_fusion
  3.5 18.2 %all-to-all-start = ((bf16[64,8,128]{2,1,0:T(8,128)(2,1)}), bf16[64,8,128]{2,1,0:T(8,128)(2,1)S(1)}, u32[]{:S(2)}, u32[]{:S(2)}) async-start(bf16[64,8,128]{2,1,0:T(8,128)(2,1)} %reshape.49), calls=%async_computation | async-start | bytes 262144 | tf_op jit(solution)/shard_map/all_to_all | solution.py:28
  21.7 1.8 %constant_dynamic-slice_fusion = bf16[512,2048]{1,0:T(8,128)(2,1)S(1)} fusion(bf16[1024,2048]{1,0:T(8,128)(2,1)} %param.6, s32[]{:T(128)S(6)} %select_n.75), kind=kLoop, calls=%fused_computation.55 | loop fusion | bytes 4194308 | tf_op jit(solution)/shard_map/dynamic_slice | solution.py:92
  23.5 3.3 %collective-permute-start.9 = (bf16[512,2048]{1,0:T(8,128)(2,1)S(1)}, bf16[512,2048]{1,0:T(8,128)(2,1)}, u32[]{:S(2)}, u32[]{:S(2)}) collective-permute-start(bf16[512,2048]{1,0:T(8,128)(2,1)S(1)} %constant_dynamic-slice_fusion), channel_id=1, source_target_pairs={{0,16},{16,0},{1,17},{17,1},{2,18},{18,2},{3,19},{19,3},{4,20},{20... | collective-permute-start | bytes 6291464 | tf_op jit(solution)/shard_map/ppermute | solution.py:20
  26.8 7.0 %all-to-all-done = bf16[64,8,128]{2,1,0:T(8,128)(2,1)S(1)} async-done(((bf16[64,8,128]{2,1,0:T(8,128)(2,1)}), bf16[64,8,128]{2,1,0:T(8,128)(2,1)S(1)}, u32[]{:S(2)}, u32[]{:S(2)}) %all-to-all-start) | async-done | bytes 131104 | tf_op jit(solution)/shard_map/all_to_all | solution.py:28
  34.4 1.1 broadcast_in_dim.2
  35.5 12.7 %all-to-all-start.1 = ((bf16[8,16,4096]{2,1,0:T(8,128)(2,1)}), bf16[8,16,4096]{2,1,0:T(8,128)(2,1)S(1)}, u32[]{:S(2)}, u32[]{:S(2)}) async-start(bf16[8,16,4096]{2,1,0:T(8,128)(2,1)} %broadcast_in_dim.2), calls=%async_computation.1 | async-start | bytes 2097152 | tf_op jit(solution)/shard_map/all_to_all | solution.py:28
  48.2 2.3 %collective-permute-start = (bf16[1,128,256]{2,1,0:T(8,128)(2,1)S(1)}, bf16[1,128,256]{2,1,0:T(8,128)(2,1)S(1)}, u32[]{:S(2)}, u32[]{:S(2)}) collective-permute-start(bf16[1,128,256]{2,1,0:T(8,128)(2,1)S(1)} %constant_dynamic-slice_fusion.1), channel_id=1, source_target_pairs={{0,8},{8,0},{1,9},{9,1},{2,10},{10,2},{3,11},{11,3},{4,12},{12,4},... | collective-permute-start | bytes 196616 | tf_op jit(solution)/shard_map/ppermute | solution.py:20
  50.6 23.4 %collective-permute-done.9 = bf16[512,2048]{1,0:T(8,128)(2,1)} collective-permute-done((bf16[512,2048]{1,0:T(8,128)(2,1)S(1)}, bf16[512,2048]{1,0:T(8,128)(2,1)}, u32[]{:S(2)}, u32[]{:S(2)}) %collective-permute-start.9) | collective-permute-done | bytes 2097184 | tf_op jit(solution)/shard_map/ppermute | solution.py:20
  73.9 2.9 %collective-permute-start.10 = (bf16[512,2048]{1,0:T(8,128)(2,1)}, bf16[512,2048]{1,0:T(8,128)(2,1)}, u32[]{:S(2)}, u32[]{:S(2)}) collective-permute-start(bf16[512,2048]{1,0:T(8,128)(2,1)} %collective-permute-done.9), channel_id=1, source_target_pairs={{0,128},{128,0},{1,129},{129,1},{2,130},{130,2},{3,131},{131,3},{4... | collective-permute-start | bytes 6291464 | tf_op jit(solution)/shard_map/ppermute | solution.py:20
  76.9 10.7 %collective-permute-start.7 = (bf16[2,128,256]{2,1,0:T(8,128)(2,1)S(1)}, bf16[2,128,256]{2,1,0:T(8,128)(2,1)S(1)}, u32[]{:S(2)}, u32[]{:S(2)}) collective-permute-start(bf16[2,128,256]{2,1,0:T(8,128)(2,1)S(1)} %pad_maximum_fusion.11.refs_0_), channel_id=1, source_target_pairs={{0,4},{1,5},{2,6},{3,7},{4,0},{5,1},{6,2},{7,3},{8,12},{9,13},{10,... | collective-permute-start | bytes 393224 | tf_op jit(solution)/shard_map/ppermute | solution.py:16
  87.6 4.7 %collective-permute-start.6 = (bf16[2,128,256]{2,1,0:T(8,128)(2,1)S(1)}, bf16[2,128,256]{2,1,0:T(8,128)(2,1)}, u32[]{:S(2)}, u32[]{:S(2)}) collective-permute-start(bf16[2,128,256]{2,1,0:T(8,128)(2,1)S(1)} %pad_maximum_fusion.11.refs_0_), channel_id=1, source_target_pairs={{0,7},{1,0},{2,1},{3,2},{4,3},{5,4},{6,5},{7,6},{8,15},{9,8},{10,9... | collective-permute-start | bytes 393224 | tf_op jit(solution)/shard_map/ppermute | solution.py:16
  92.3 1.9 %collective-permute-start.5 = (bf16[2,128,256]{2,1,0:T(8,128)(2,1)S(1)}, bf16[2,128,256]{2,1,0:T(8,128)(2,1)}, u32[]{:S(2)}, u32[]{:S(2)}) collective-permute-start(bf16[2,128,256]{2,1,0:T(8,128)(2,1)S(1)} %pad_maximum_fusion.11.refs_0_), channel_id=1, source_target_pairs={{0,1},{1,2},{2,3},{3,4},{4,5},{5,6},{6,7},{7,0},{8,9},{9,10},{10,1... | collective-permute-start | bytes 393224 | tf_op jit(solution)/shard_map/ppermute | solution.py:16
  94.2 3.1 %collective-permute-start.4 = (bf16[2,128,256]{2,1,0:T(8,128)(2,1)S(1)}, bf16[2,128,256]{2,1,0:T(8,128)(2,1)}, u32[]{:S(2)}, u32[]{:S(2)}) collective-permute-start(bf16[2,128,256]{2,1,0:T(8,128)(2,1)S(1)} %pad_maximum_fusion.11.refs_0_), channel_id=1, source_target_pairs={{0,6},{1,7},{2,0},{3,1},{4,2},{5,3},{6,4},{7,5},{8,14},{9,15},{10,... | collective-permute-start | bytes 393224 | tf_op jit(solution)/shard_map/ppermute | solution.py:16
  97.3 2.1 %collective-permute-start.11 = (bf16[8,16,4096]{2,1,0:T(8,128)(2,1)S(1)}, bf16[8,16,4096]{2,1,0:T(8,128)(2,1)}, u32[]{:S(2)}, u32[]{:S(2)}) collective-permute-start(bf16[8,16,4096]{2,1,0:T(8,128)(2,1)S(1)} %all-to-all-done.1), channel_id=1, source_target_pairs={{0,8},{8,0},{1,9},{9,1},{2,10},{10,2},{3,11},{11,3},{4,12},{12,4},... | collective-permute-start | bytes 3145736 | tf_op jit(solution)/shard_map/ppermute | solution.py:20
  99.4 4.0 %collective-permute-start.3 = (bf16[2,128,256]{2,1,0:T(8,128)(2,1)S(1)}, bf16[2,128,256]{2,1,0:T(8,128)(2,1)}, u32[]{:S(2)}, u32[]{:S(2)}) collective-permute-start(bf16[2,128,256]{2,1,0:T(8,128)(2,1)S(1)} %pad_maximum_fusion.11.refs_0_), channel_id=1, source_target_pairs={{0,2},{1,3},{2,4},{3,5},{4,6},{5,7},{6,0},{7,1},{8,10},{9,11},{10,... | collective-permute-start | bytes 393224 | tf_op jit(solution)/shard_map/ppermute | solution.py:16
  103.4 6.7 %collective-permute-start.2 = (bf16[2,128,256]{2,1,0:T(8,128)(2,1)S(1)}, bf16[2,128,256]{2,1,0:T(8,128)(2,1)}, u32[]{:S(2)}, u32[]{:S(2)}) collective-permute-start(bf16[2,128,256]{2,1,0:T(8,128)(2,1)S(1)} %pad_maximum_fusion.11.refs_0_), channel_id=1, source_target_pairs={{0,5},{1,6},{2,7},{3,0},{4,1},{5,2},{6,3},{7,4},{8,13},{9,14},{10,... | collective-permute-start | bytes 393224 | tf_op jit(solution)/shard_map/ppermute | solution.py:16
  110.1 3.1 %collective-permute-start.1 = (bf16[2,128,256]{2,1,0:T(8,128)(2,1)S(1)}, bf16[2,128,256]{2,1,0:T(8,128)(2,1)}, u32[]{:S(2)}, u32[]{:S(2)}) collective-permute-start(bf16[2,128,256]{2,1,0:T(8,128)(2,1)S(1)} %pad_maximum_fusion.11.refs_0_), channel_id=1, source_target_pairs={{0,3},{1,4},{2,5},{3,6},{4,7},{5,0},{6,1},{7,2},{8,11},{9,12},{10,... | collective-permute-start | bytes 393224 | tf_op jit(solution)/shard_map/ppermute | solution.py:16
  113.3 6.1 %collective-permute-done.2.refs_2_ = bf16[2,128,256]{2,1,0:T(8,128)(2,1)} collective-permute-done((bf16[2,128,256]{2,1,0:T(8,128)(2,1)S(1)}, bf16[2,128,256]{2,1,0:T(8,128)(2,1)}, u32[]{:S(2)}, u32[]{:S(2)}) %collective-permute-start.2) | collective-permute-done | bytes 131104 | tf_op jit(solution)/shard_map/ppermute | solution.py:16
  119.4 2.6 %collective-permute-done.1.refs_1_ = bf16[2,128,256]{2,1,0:T(8,128)(2,1)} collective-permute-done((bf16[2,128,256]{2,1,0:T(8,128)(2,1)S(1)}, bf16[2,128,256]{2,1,0:T(8,128)(2,1)}, u32[]{:S(2)}, u32[]{:S(2)}) %collective-permute-start.1) | collective-permute-done | bytes 131104 | tf_op jit(solution)/shard_map/ppermute | solution.py:16
  122.1 2.3 %join.1 = bf16[16,128,256]{2,1,0:T(8,128)(2,1)} custom-call(bf16[2,128,256]{2,1,0:T(8,128)(2,1)} %copy-done.3, bf16[2,128,256]{2,1,0:T(8,128)(2,1)} %collective-permute-done.1.refs_1_, bf16[2,128,256]{2,1,0:T(8,128)(2,1)} %collective-permute-done.2.refs_2_, bf16[2,128,256]{2,1,0:T(8,128)(2,1)} %collective-permute-done.3.refs_3_, ...), custom_call_target="tpu_custom_call" | custom-call | bytes 2097152 | tf_op jit(solution)/shard_map/join/pallas_call | solution.py:46
  124.4 2.7 %collective-permute-start.8 = (bf16[16,128,256]{2,1,0:T(8,128)(2,1)}, bf16[16,128,256]{2,1,0:T(8,128)(2,1)}, u32[]{:S(2)}, u32[]{:S(2)}) collective-permute-start(bf16[16,128,256]{2,1,0:T(8,128)(2,1)} %join.1), channel_id=1, source_target_pairs={{0,128},{128,0},{1,129},{129,1},{2,130},{130,2},{3,131},{131,3},{4... | collective-permute-start | bytes 3145736 | tf_op jit(solution)/shard_map/ppermute | solution.py:20
  127.2 2.4 %fusion.6 = f32[128,512]{1,0:T(8,128)S(1)} fusion(bf16[1024,2048]{1,0:T(8,128)(2,1)} %param.6, s32[]{:T(128)S(6)} %select_n.76, bf16[128,4096]{1,0:T(8,128)(2,1)S(1)} %bitcast.41), kind=kOutput, calls=%fused_computation.6 | convolution fusion | flops 268435456 | bytes 2883588 | tf_op jit(solution)/shard_map/dot_general | solution.py:57
  130.4 2.4 %fusion.11 = bf16[128,512]{1,0:T(8,128)(2,1)S(1)} fusion(f32[128,512]{1,0:T(8,128)S(1)} %fusion.23, bf16[512,2048]{1,0:T(8,128)(2,1)} %collective-permute-done.9, bf16[128,4096]{1,0:T(8,128)(2,1)S(1)} %bitcast.43), kind=kOutput, calls=%fused_computation.13 | convolution fusion | flops 268566528 | bytes 3014656 | tf_op jit(solution)/shard_map/dot_general | solution.py:57
  132.9 2.0 %fusion.18 = f32[128,512]{1,0:T(8,128)S(1)} fusion(bf16[512,2048]{1,0:T(8,128)(2,1)S(1)} %constant_dynamic-slice_fusion, bf16[128,4096]{1,0:T(8,128)(2,1)} %bitcast.9), kind=kOutput, calls=%fused_computation.22 | convolution fusion | flops 268435456 | bytes 2883584 | tf_op jit(solution)/shard_map/dot_general | solution.py:57
  134.9 2.6 %fusion.13 = bf16[128,512]{1,0:T(8,128)(2,1)S(1)} fusion(f32[128,512]{1,0:T(8,128)S(1)} %fusion.18, bf16[512,2048]{1,0:T(8,128)(2,1)} %collective-permute-done.9, bf16[128,4096]{1,0:T(8,128)(2,1)} %bitcast.9), kind=kOutput, calls=%fused_computation.15 | convolution fusion | flops 268566528 | bytes 3014656 | tf_op jit(solution)/shard_map/dot_general | solution.py:57
  137.5 1.9 %fusion.4 = f32[128,512]{1,0:T(8,128)S(1)} fusion(bf16[1024,2048]{1,0:T(8,128)(2,1)S(1)} %copy-done.1, s32[]{:T(128)S(6)} %select_n.76, bf16[128,4096]{1,0:T(8,128)(2,1)} %bitcast.9), kind=kOutput, calls=%fused_computation.4 | convolution fusion | flops 268435456 | bytes 2883588 | tf_op jit(solution)/shard_map/dot_general | solution.py:57
  139.4 2.6 %fusion.14 = bf16[128,512]{1,0:T(8,128)(2,1)S(1)} fusion(f32[128,512]{1,0:T(8,128)S(1)} %fusion.4, bf16[512,2048]{1,0:T(8,128)(2,1)} %collective-permute-done.10, bf16[128,4096]{1,0:T(8,128)(2,1)} %bitcast.9), kind=kOutput, calls=%fused_computation.16 | convolution fusion | flops 268566528 | bytes 3014656 | tf_op jit(solution)/shard_map/dot_general | solution.py:57
  142.1 2.4 %fusion.12 = bf16[128,512]{1,0:T(8,128)(2,1)S(1)} fusion(f32[128,512]{1,0:T(8,128)S(1)} %fusion.6, bf16[512,2048]{1,0:T(8,128)(2,1)} %collective-permute-done.10, bf16[128,4096]{1,0:T(8,128)(2,1)S(1)} %bitcast.44), kind=kOutput, calls=%fused_computation.14 | convolution fusion | flops 268566528 | bytes 3014656 | tf_op jit(solution)/shard_map/dot_general | solution.py:57
  145.5 5.9 %all-to-all-start.2 = ((bf16[8,32,1024]{2,1,0:T(8,128)(2,1)}), bf16[8,32,1024]{2,1,0:T(8,128)(2,1)S(1)}, u32[]{:S(2)}, u32[]{:S(2)}) async-start(bf16[8,32,1024]{2,1,0:T(8,128)(2,1)} %pad_maximum_fusion.7), calls=%async_computation.2 | async-start | bytes 1048576 | tf_op jit(solution)/shard_map/all_to_all | solution.py:28
  151.4 3.0 %fusion.8 = bf16[256,256]{1,0:T(8,128)(2,1)S(1)} fusion(bf16[16,128,256]{2,1,0:T(8,128)(2,1)} %collective-permute-done.8, bf16[16,128,256]{2,1,0:T(8,128)(2,1)S(1)} %copy-done.2, bf16[1,1,256,256]{3,2,1,0:T(8,128)(2,1)S(1)} %copy-done), kind=kOutput, calls=%fused_computation.12 | convolution fusion | flops 1083179008 | bytes 2359296 | tf_op jit(solution)/shard_map/pad,pbd->ab/dot_general | solution.py:116
  155.2 14.3 %all-to-all-done.2 = bf16[8,32,1024]{2,1,0:T(8,128)(2,1)S(1)} async-done(((bf16[8,32,1024]{2,1,0:T(8,128)(2,1)}), bf16[8,32,1024]{2,1,0:T(8,128)(2,1)S(1)}, u32[]{:S(2)}, u32[]{:S(2)}) %all-to-all-start.2) | async-done | bytes 524320 | tf_op jit(solution)/shard_map/all_to_all | solution.py:28
  (42 shorter events, 5.8 us)
Async XLA Ops:
  0.6 0.9 copy-start
  3.5 30.3 %all-to-all-start = ((bf16[64,8,128]{2,1,0:T(8,128)(2,1)}), bf16[64,8,128]{2,1,0:T(8,128)(2,1)S(1)}, u32[]{:S(2)}, u32[]{:S(2)}) async-start(bf16[64,8,128]{2,1,0:T(8,128)(2,1)} %reshape.49), calls=%async_computation | async-start | bytes 262144 | tf_op jit(solution)/shard_map/all_to_all | solution.py:28
  23.5 50.4 %collective-permute-start.9 = (bf16[512,2048]{1,0:T(8,128)(2,1)S(1)}, bf16[512,2048]{1,0:T(8,128)(2,1)}, u32[]{:S(2)}, u32[]{:S(2)}) collective-permute-start(bf16[512,2048]{1,0:T(8,128)(2,1)S(1)} %constant_dynamic-slice_fusion), channel_id=1, source_target_pairs={{0,16},{16,0},{1,17},{17,1},{2,18},{18,2},{3,19},{19,3},{4,20},{20... | collective-permute-start | bytes 6291464 | tf_op jit(solution)/shard_map/ppermute | solution.py:20
  34.0 14.2 %copy-start.5 = (bf16[1,256,256]{2,1,0:T(8,128)(2,1)S(1)}, bf16[1,256,256]{2,1,0:T(8,128)(2,1)}, u32[]{:S(2)}) copy-start(bf16[1,256,256]{2,1,0:T(8,128)(2,1)} %param.5) | copy-start | bytes 393220
  35.5 61.8 %all-to-all-start.1 = ((bf16[8,16,4096]{2,1,0:T(8,128)(2,1)}), bf16[8,16,4096]{2,1,0:T(8,128)(2,1)S(1)}, u32[]{:S(2)}, u32[]{:S(2)}) async-start(bf16[8,16,4096]{2,1,0:T(8,128)(2,1)} %broadcast_in_dim.2), calls=%async_computation.1 | async-start | bytes 2097152 | tf_op jit(solution)/shard_map/all_to_all | solution.py:28
  48.2 28.6 %collective-permute-start = (bf16[1,128,256]{2,1,0:T(8,128)(2,1)S(1)}, bf16[1,128,256]{2,1,0:T(8,128)(2,1)S(1)}, u32[]{:S(2)}, u32[]{:S(2)}) collective-permute-start(bf16[1,128,256]{2,1,0:T(8,128)(2,1)S(1)} %constant_dynamic-slice_fusion.1), channel_id=1, source_target_pairs={{0,8},{8,0},{1,9},{9,1},{2,10},{10,2},{3,11},{11,3},{4,12},{12,4},... | collective-permute-start | bytes 196616 | tf_op jit(solution)/shard_map/ppermute | solution.py:20
  73.9 65.5 %collective-permute-start.10 = (bf16[512,2048]{1,0:T(8,128)(2,1)}, bf16[512,2048]{1,0:T(8,128)(2,1)}, u32[]{:S(2)}, u32[]{:S(2)}) collective-permute-start(bf16[512,2048]{1,0:T(8,128)(2,1)} %collective-permute-done.9), channel_id=1, source_target_pairs={{0,128},{128,0},{1,129},{129,1},{2,130},{130,2},{3,131},{131,3},{4... | collective-permute-start | bytes 6291464 | tf_op jit(solution)/shard_map/ppermute | solution.py:20
  76.9 45.2 %copy-start.3 = (bf16[2,128,256]{2,1,0:T(8,128)(2,1)}, bf16[2,128,256]{2,1,0:T(8,128)(2,1)S(1)}, u32[]{:S(2)}) copy-start(bf16[2,128,256]{2,1,0:T(8,128)(2,1)S(1)} %pad_maximum_fusion.11.refs_0_) | copy-start | bytes 393220
  76.9 20.4 %collective-permute-start.7 = (bf16[2,128,256]{2,1,0:T(8,128)(2,1)S(1)}, bf16[2,128,256]{2,1,0:T(8,128)(2,1)S(1)}, u32[]{:S(2)}, u32[]{:S(2)}) collective-permute-start(bf16[2,128,256]{2,1,0:T(8,128)(2,1)S(1)} %pad_maximum_fusion.11.refs_0_), channel_id=1, source_target_pairs={{0,4},{1,5},{2,6},{3,7},{4,0},{5,1},{6,2},{7,3},{8,12},{9,13},{10,... | collective-permute-start | bytes 393224 | tf_op jit(solution)/shard_map/ppermute | solution.py:16
  87.6 11.8 %collective-permute-start.6 = (bf16[2,128,256]{2,1,0:T(8,128)(2,1)S(1)}, bf16[2,128,256]{2,1,0:T(8,128)(2,1)}, u32[]{:S(2)}, u32[]{:S(2)}) collective-permute-start(bf16[2,128,256]{2,1,0:T(8,128)(2,1)S(1)} %pad_maximum_fusion.11.refs_0_), channel_id=1, source_target_pairs={{0,7},{1,0},{2,1},{3,2},{4,3},{5,4},{6,5},{7,6},{8,15},{9,8},{10,9... | collective-permute-start | bytes 393224 | tf_op jit(solution)/shard_map/ppermute | solution.py:16
  92.3 11.2 %collective-permute-start.5 = (bf16[2,128,256]{2,1,0:T(8,128)(2,1)S(1)}, bf16[2,128,256]{2,1,0:T(8,128)(2,1)}, u32[]{:S(2)}, u32[]{:S(2)}) collective-permute-start(bf16[2,128,256]{2,1,0:T(8,128)(2,1)S(1)} %pad_maximum_fusion.11.refs_0_), channel_id=1, source_target_pairs={{0,1},{1,2},{2,3},{3,4},{4,5},{5,6},{6,7},{7,0},{8,9},{9,10},{10,1... | collective-permute-start | bytes 393224 | tf_op jit(solution)/shard_map/ppermute | solution.py:16
  94.2 15.9 %collective-permute-start.4 = (bf16[2,128,256]{2,1,0:T(8,128)(2,1)S(1)}, bf16[2,128,256]{2,1,0:T(8,128)(2,1)}, u32[]{:S(2)}, u32[]{:S(2)}) collective-permute-start(bf16[2,128,256]{2,1,0:T(8,128)(2,1)S(1)} %pad_maximum_fusion.11.refs_0_), channel_id=1, source_target_pairs={{0,6},{1,7},{2,0},{3,1},{4,2},{5,3},{6,4},{7,5},{8,14},{9,15},{10,... | collective-permute-start | bytes 393224 | tf_op jit(solution)/shard_map/ppermute | solution.py:16
  97.3 24.7 %copy-start.4 = (bf16[2,128,256]{2,1,0:T(8,128)(2,1)}, bf16[2,128,256]{2,1,0:T(8,128)(2,1)S(1)}, u32[]{:S(2)}) copy-start(bf16[2,128,256]{2,1,0:T(8,128)(2,1)S(1)} %collective-permute-done.7.refs_7_) | copy-start | bytes 393220
  97.3 35.5 %collective-permute-start.11 = (bf16[8,16,4096]{2,1,0:T(8,128)(2,1)S(1)}, bf16[8,16,4096]{2,1,0:T(8,128)(2,1)}, u32[]{:S(2)}, u32[]{:S(2)}) collective-permute-start(bf16[8,16,4096]{2,1,0:T(8,128)(2,1)S(1)} %all-to-all-done.1), channel_id=1, source_target_pairs={{0,8},{8,0},{1,9},{9,1},{2,10},{10,2},{3,11},{11,3},{4,12},{12,4},... | collective-permute-start | bytes 3145736 | tf_op jit(solution)/shard_map/ppermute | solution.py:20
  99.4 13.8 %collective-permute-start.3 = (bf16[2,128,256]{2,1,0:T(8,128)(2,1)S(1)}, bf16[2,128,256]{2,1,0:T(8,128)(2,1)}, u32[]{:S(2)}, u32[]{:S(2)}) collective-permute-start(bf16[2,128,256]{2,1,0:T(8,128)(2,1)S(1)} %pad_maximum_fusion.11.refs_0_), channel_id=1, source_target_pairs={{0,2},{1,3},{2,4},{3,5},{4,6},{5,7},{6,0},{7,1},{8,10},{9,11},{10,... | collective-permute-start | bytes 393224 | tf_op jit(solution)/shard_map/ppermute | solution.py:16
  103.4 16.0 %collective-permute-start.2 = (bf16[2,128,256]{2,1,0:T(8,128)(2,1)S(1)}, bf16[2,128,256]{2,1,0:T(8,128)(2,1)}, u32[]{:S(2)}, u32[]{:S(2)}) collective-permute-start(bf16[2,128,256]{2,1,0:T(8,128)(2,1)S(1)} %pad_maximum_fusion.11.refs_0_), channel_id=1, source_target_pairs={{0,5},{1,6},{2,7},{3,0},{4,1},{5,2},{6,3},{7,4},{8,13},{9,14},{10,... | collective-permute-start | bytes 393224 | tf_op jit(solution)/shard_map/ppermute | solution.py:16
  110.1 11.9 %collective-permute-start.1 = (bf16[2,128,256]{2,1,0:T(8,128)(2,1)S(1)}, bf16[2,128,256]{2,1,0:T(8,128)(2,1)}, u32[]{:S(2)}, u32[]{:S(2)}) collective-permute-start(bf16[2,128,256]{2,1,0:T(8,128)(2,1)S(1)} %pad_maximum_fusion.11.refs_0_), channel_id=1, source_target_pairs={{0,3},{1,4},{2,5},{3,6},{4,7},{5,0},{6,1},{7,2},{8,11},{9,12},{10,... | collective-permute-start | bytes 393224 | tf_op jit(solution)/shard_map/ppermute | solution.py:16
  124.4 27.0 %collective-permute-start.8 = (bf16[16,128,256]{2,1,0:T(8,128)(2,1)}, bf16[16,128,256]{2,1,0:T(8,128)(2,1)}, u32[]{:S(2)}, u32[]{:S(2)}) collective-permute-start(bf16[16,128,256]{2,1,0:T(8,128)(2,1)} %join.1), channel_id=1, source_target_pairs={{0,128},{128,0},{1,129},{129,1},{2,130},{130,2},{3,131},{131,3},{4... | collective-permute-start | bytes 3145736 | tf_op jit(solution)/shard_map/ppermute | solution.py:20
  132.9 4.7 %copy-start.1 = (bf16[1024,2048]{1,0:T(8,128)(2,1)S(1)}, bf16[1024,2048]{1,0:T(8,128)(2,1)}, u32[]{:S(2)}) copy-start(bf16[1024,2048]{1,0:T(8,128)(2,1)} %param.6) | copy-start | bytes 12582916
  144.5 6.9 %copy-start.2 = (bf16[16,128,256]{2,1,0:T(8,128)(2,1)S(1)}, bf16[16,128,256]{2,1,0:T(8,128)(2,1)}, u32[]{:S(2)}) copy-start(bf16[16,128,256]{2,1,0:T(8,128)(2,1)} %join.1) | copy-start | bytes 3145732
  145.5 24.0 %all-to-all-start.2 = ((bf16[8,32,1024]{2,1,0:T(8,128)(2,1)}), bf16[8,32,1024]{2,1,0:T(8,128)(2,1)S(1)}, u32[]{:S(2)}, u32[]{:S(2)}) async-start(bf16[8,32,1024]{2,1,0:T(8,128)(2,1)} %pad_maximum_fusion.7), calls=%async_computation.2 | async-start | bytes 1048576 | tf_op jit(solution)/shard_map/all_to_all | solution.py:28
where the time goes:
time: 171 us; the launch traced here: 170 us
  starting transfers between devices  84.3 us (49%)
  waiting for transfers between devices  53.4 us (31%)
  matrix products  21.1 us (12%)
  local copies, waits for them, and re-layouts  5.47 us (3%)
  other arithmetic  2.47 us (1%)
  Pallas kernels  2.34 us (1%)
    all_to_all x3, starting transfers between devices, exchange(): return lax.all_to_all(x, axes, 0, 0, tiled=True)  36.8 us
    ppermute x7, starting transfers between devices, shift(): return lax.ppermute(x, 'z', [(i, (i + by) % depth) for i in range(depth)])  34.2 us
    ppermute x5, waiting for transfers between devices, swap(): return lax.ppermute(x, axis, [(0, 1), (1, 0)])  23.4 us
    all_to_all x3, waiting for transfers between devices, exchange(): return lax.all_to_all(x, axes, 0, 0, tiled=True)  21.3 us
    dot_general x8, matrix products, product(): lax.dot_general(panel, weight, (((1,), (1,)), ((), ())), preferred_elemen...  17.2 us
    ppermute x5, starting transfers between devices, swap(): return lax.ppermute(x, axis, [(0, 1), (1, 0)])  13.3 us
    ppermute x7, waiting for transfers between devices, shift(): return lax.ppermute(x, 'z', [(i, (i + by) % depth) for i in range(depth)])  8.81 us
  transfers between devices with their start and end apart: 15, of which 5 were waited for; matrix products, arithmetic and copies ran while one was open for 15% of the time, Pallas kernels for 1%

commit v1 on v0

--- a/solution.py
+++ b/solution.py
@@ -5,6 +5,7 @@
 from jax.experimental.pallas import tpu as pltpu
 from jax.sharding import Mesh, PartitionSpec as P
 
+VMEM = 20 * 1024 * 1024
 AXES = ("hi", "core", "rowpair", "side", "lo", "z")
 
 
@@ -28,11 +29,6 @@
     return lax.all_to_all(x, axes, 0, 0, tiled=True)
 
 
-def in_order(mine, other, axis, dim):
-    first = lax.axis_index(axis) == 0
-    return jnp.concatenate([jnp.where(first, mine, other), jnp.where(first, other, mine)], axis=dim)
-
-
 def join_kernel(*refs):
     pieces, out_ref = refs[:-1], refs[-1]
     count = pieces[0].shape[0]
@@ -49,21 +45,45 @@
         out_specs=pl.BlockSpec(memory_space=pltpu.VMEM),
         out_shape=jax.ShapeDtypeStruct(shape, blocks[0].dtype),
         cost_estimate=pl.CostEstimate(flops=0, bytes_accessed=size, transcendentals=0),
+        compiler_params=pltpu.CompilerParams(vmem_limit_bytes=VMEM),
         name="join",
     )(*blocks)
 
 
-def product(panel, weight):
-    return lax.dot_general(panel, weight, (((1,), (1,)), ((), ())), preferred_element_type=jnp.float32)
+def product_kernel(near_ref, far_ref, weight_ref, near_other_ref, last_other_ref, out_ref, own_ref, sems):
+    core, low = lax.axis_index("core"), lax.axis_index("lo")
+    count = near_ref.shape[0]
+    part, inner = near_other_ref.shape
+    halves = [pl.ds(pl.multiple_of(at * part, part), part) for at in (core, 1 - core)]
+    copies = [pltpu.make_async_copy(weight_ref.at[rows], own_ref.at[i], sems.at[i]) for i, rows in enumerate(halves)]
+    for copy in copies:
+        copy.start()
+
+    def term(weight, at):
+        panel = jnp.concatenate([near_ref[:, at : at + inner], far_ref[:, at : at + inner]], axis=0)
+        return lax.dot_general(weight, panel, (((1,), (1,)), ((), ())), preferred_element_type=jnp.float32)
+
+    others = [term(ref[...], inner) for ref in (near_other_ref, last_other_ref)]
+    for i, rows in enumerate(halves):
+        copies[i].wait()
+        sums = (term(own_ref[i], 0) + others[i]).T.astype(out_ref.dtype)
+        out_ref[pl.ds(pl.multiple_of(low * count, count), count), rows] = sums[:count]
+        out_ref[pl.ds(pl.multiple_of((1 - low) * count, count), count), rows] = sums[count:]
 
 
-def sums_of(panel, weights):
-    panel = panel.reshape(-1, panel.shape[-1])
-    inner = panel.shape[1] // 2
-    here, there = panel[:, :inner], panel[:, inner:]
-    return jnp.concatenate(
-        [(product(here, a) + product(there, b)).astype(jnp.bfloat16) for a, b in weights], axis=1
-    )
+def products(near, far, *weights):
+    count, outs = near.shape[0], weights[0].shape[0]
+    flops = 4 * near.size * outs
+    return pl.pallas_call(
+        product_kernel,
+        in_specs=[pl.BlockSpec(memory_space=pl.ANY if i == 2 else pltpu.VMEM) for i in range(5)],
+        out_specs=pl.BlockSpec(memory_space=pltpu.VMEM),
+        out_shape=jax.ShapeDtypeStruct((2 * count, outs), jnp.bfloat16),
+        scratch_shapes=[pltpu.VMEM((2, outs // 2, near.shape[1] // 2), jnp.bfloat16), pltpu.SemaphoreType.DMA((2,))],
+        cost_estimate=pl.CostEstimate(flops=flops, bytes_accessed=8 * outs * near.shape[1], transcendentals=0),
+        compiler_params=pltpu.CompilerParams(vmem_limit_bytes=44 * 1024 * 1024),
+        name="products",
+    )(near, far, *weights)
 
 
 def body(amplitudes, factors, cycle_weight, orbital_order):
@@ -90,7 +110,6 @@
 
     part = outs // 2
     near_weight = lax.dynamic_slice_in_dim(cycle_weight, core * part, part, axis=0)
-    last_weight = lax.dynamic_slice_in_dim(cycle_weight, (1 - core) * part, part, axis=0)
     near_other = swap(near_weight, "side")
     last_other = swap(near_other, "core")
 
@@ -104,10 +123,8 @@
     blocks = [both] + [shift(both, by) for by in SHIFTS]
 
     far = swap(near, "lo")
-    weights = ((near_weight, near_other), (last_weight, last_other))
-    near_sums = sums_of(near, weights)
-    far_sums = sums_of(tied(far, near_sums), weights)
-    parts = in_order(near_sums.reshape(pairs, -1, outs), far_sums.reshape(pairs, -1, outs), "lo", 0)
+    near, far = near.reshape(depth * width, -1), far.reshape(depth * width, -1)
+    parts = products(near, far, cycle_weight, near_other, last_other).reshape(2 * pairs, -1, outs)
     parts = exchange(parts, ("rowpair", "side"))
     halves = joined(blocks)
     others = swap(halves, "core")
@@ -118,8 +135,7 @@
     ladder_term = jnp.where(core == 0, ladder, swapped).astype(jnp.bfloat16).reshape(amplitudes.shape)
     parts = tied(parts, ladder_term)
     total = jnp.sum(parts.reshape(pairs, 2, 2, width, outs).astype(jnp.float32), axis=0)
-    total = jnp.transpose(total, (1, 0, 2, 3)).reshape(4 * width, outs).astype(jnp.bfloat16)
-    cycle_term = in_order(total[:, :part], total[:, part:], "core", 1)
+    cycle_term = jnp.transpose(total, (1, 0, 2, 3)).reshape(4 * width, outs).astype(jnp.bfloat16)
 
     return (ladder_term, cycle_term)
 

time: 171 us -> 173 us (1.012)
  matrix products: 21.1 us -> 3.77 us
  waiting for transfers between devices: 53.4 us -> 70.1 us
  Pallas kernels: 2.34 us -> 8.3 us
  starting transfers between devices: 84.3 us -> 81.1 us
  local copies, waits for them, and re-layouts: 5.47 us -> 7.35 us
    all_to_all x3, waiting for transfers between devices: 21.3 us -> 50.5 us  [exchange(): return lax.all_to_all(x, axes, 0, 0, tiled=True)]
    ppermute x5, waiting for transfers between devices: 23.4 us -> 2.41 us  [swap(): return lax.ppermute(x, axis, [(0, 1), (1, 0)])]
    dot_general x8 -> x0, matrix products: 17.2 us -> none  [product(): lax.dot_general(panel, weight, (((1,), (1,)), ((), ())), preferred_elemen...]
    ppermute x7, starting transfers between devices: 34.2 us -> 24 us  [shift(): return lax.ppermute(x, 'z', [(i, (i + by) % depth) for i in range(depth)])]
    ppermute x7, waiting for transfers between devices: 8.81 us -> 17.2 us  [shift(): return lax.ppermute(x, 'z', [(i, (i + by) % depth) for i in range(depth)])]
    ppermute x5, starting transfers between devices: 13.3 us -> 21.2 us  [swap(): return lax.ppermute(x, axis, [(0, 1), (1, 0)])]
    pallas_call x0 -> x1, Pallas kernels: none -> 6.22 us  [products(): pl.pallas_call(product_kernel, in_specs=[pl.BlockSpec(memory_space=pl.ANY...]
  transfers between devices with their start and end apart: 15 -> 15, of which waited for: 5 -> 7; matrix products, arithmetic and copies ran while one was open for 15% -> 4% of each run, Pallas kernels for 1% -> 5%
where the time goes in v1:
time: 173 us; the launch traced here: 172 us
  starting transfers between devices  81.1 us (47%)
  waiting for transfers between devices  70.1 us (41%)
  Pallas kernels  8.3 us (5%)
  local copies, waits for them, and re-layouts  7.35 us (4%)
  matrix products  3.77 us (2%)
    all_to_all x3, waiting for transfers between devices, exchange(): return lax.all_to_all(x, axes, 0, 0, tiled=True)  50.5 us
    all_to_all x3, starting transfers between devices, exchange(): return lax.all_to_all(x, axes, 0, 0, tiled=True)  35.9 us
    ppermute x7, starting transfers between devices, shift(): return lax.ppermute(x, 'z', [(i, (i + by) % depth) for i in range(depth)])  24 us
    ppermute x5, starting transfers between devices, swap(): return lax.ppermute(x, axis, [(0, 1), (1, 0)])  21.2 us
    ppermute x7, waiting for transfers between devices, shift(): return lax.ppermute(x, 'z', [(i, (i + by) % depth) for i in range(depth)])  17.2 us
    pallas_call x1, Pallas kernels, products(): pl.pallas_call(product_kernel, in_specs=[pl.BlockSpec(memory_space=pl.ANY...  6.22 us
    dot_general x1, matrix products, body(): jnp.einsum('pad,pbd->ab', dressed, whole, preferred_element_type=jnp.floa...  3.54 us
  transfers between devices with their start and end apart: 15, of which 7 were waited for; matrix products, arithmetic and copies ran while one was open for 4% of the time, Pallas kernels for 5%

profile of v1, /device:TPU:1, one launch (start us, length us, event | category | flops | bytes accessed | tf_op | source)
XLA Modules:
  0.0 172.5 jit_solution(1039165834018813050)
XLA Ops:
  0.7 3.2 %constant_dynamic-slice_fusion = bf16[512,2048]{1,0:T(8,128)(2,1)} fusion(bf16[1024,2048]{1,0:T(8,128)(2,1)} %weight_ref.1, s32[]{:T(128)S(6)} %select_n.40), kind=kLoop, calls=%fused_computation.23 | loop fusion | bytes 4194308 | tf_op jit(solution)/shard_map/dynamic_slice | solution.py:112
  3.9 4.1 %collective-permute-start.10 = (bf16[512,2048]{1,0:T(8,128)(2,1)}, bf16[512,2048]{1,0:T(8,128)(2,1)S(1)}, u32[]{:S(2)}, u32[]{:S(2)}) collective-permute-start(bf16[512,2048]{1,0:T(8,128)(2,1)} %constant_dynamic-slice_fusion), channel_id=1, source_target_pairs={{0,16},{16,0},{1,17},{17,1},{2,18},{18,2},{3,19},{19,3},{4,20},{20... | collective-permute-start | bytes 6291464 | tf_op jit(solution)/shard_map/ppermute | solution.py:21
  8.0 0.2 convolution_convert_fusion
  8.5 0.8 reshape.46
  9.3 16.0 %all-to-all-start = ((bf16[64,8,128]{2,1,0:T(8,128)(2,1)}), bf16[64,8,128]{2,1,0:T(8,128)(2,1)S(1)}, u32[]{:S(2)}, u32[]{:S(2)}) async-start(bf16[64,8,128]{2,1,0:T(8,128)(2,1)} %reshape.46), calls=%async_computation | async-start | bytes 262144 | tf_op jit(solution)/shard_map/all_to_all | solution.py:29
  25.3 36.8 %all-to-all-done = bf16[64,8,128]{2,1,0:T(8,128)(2,1)S(1)} async-done(((bf16[64,8,128]{2,1,0:T(8,128)(2,1)}), bf16[64,8,128]{2,1,0:T(8,128)(2,1)S(1)}, u32[]{:S(2)}, u32[]{:S(2)}) %all-to-all-start) | async-done | bytes 131104 | tf_op jit(solution)/shard_map/all_to_all | solution.py:29
  62.7 1.1 broadcast_in_dim.2
  63.8 16.4 %all-to-all-start.1 = ((bf16[8,16,4096]{2,1,0:T(8,128)(2,1)}), bf16[8,16,4096]{2,1,0:T(8,128)(2,1)S(1)}, u32[]{:S(2)}, u32[]{:S(2)}) async-start(bf16[8,16,4096]{2,1,0:T(8,128)(2,1)} %broadcast_in_dim.2), calls=%async_computation.1 | async-start | bytes 2097152 | tf_op jit(solution)/shard_map/all_to_all | solution.py:29
  80.2 2.6 %collective-permute-start.11 = (bf16[512,2048]{1,0:T(8,128)(2,1)S(1)}, bf16[512,2048]{1,0:T(8,128)(2,1)}, u32[]{:S(2)}, u32[]{:S(2)}) collective-permute-start(bf16[512,2048]{1,0:T(8,128)(2,1)S(1)} %collective-permute-done.10.near_other_ref), channel_id=1, source_target_pairs={{0,128},{128,0},{1,129},{129,1},{2,130},{130,2},{3,131},{131,3},{4... | collective-permute-start | bytes 6291464 | tf_op jit(solution)/shard_map/ppermute | solution.py:21
  82.8 3.1 %collective-permute-start = (bf16[1,128,256]{2,1,0:T(8,128)(2,1)S(1)}, bf16[1,128,256]{2,1,0:T(8,128)(2,1)S(1)}, u32[]{:S(2)}, u32[]{:S(2)}) collective-permute-start(bf16[1,128,256]{2,1,0:T(8,128)(2,1)S(1)} %constant_dynamic-slice_fusion.1), channel_id=1, source_target_pairs={{0,8},{8,0},{1,9},{9,1},{2,10},{10,2},{3,11},{11,3},{4,12},{12,4},... | collective-permute-start | bytes 196616 | tf_op jit(solution)/shard_map/ppermute | solution.py:21
  86.0 2.4 %collective-permute-done = bf16[1,128,256]{2,1,0:T(8,128)(2,1)S(1)} collective-permute-done((bf16[1,128,256]{2,1,0:T(8,128)(2,1)S(1)}, bf16[1,128,256]{2,1,0:T(8,128)(2,1)S(1)}, u32[]{:S(2)}, u32[]{:S(2)}) %collective-permute-start) | collective-permute-done | bytes 65568 | tf_op jit(solution)/shard_map/ppermute | solution.py:21
  88.4 7.5 %collective-permute-start.7 = (bf16[2,128,256]{2,1,0:T(8,128)(2,1)S(1)}, bf16[2,128,256]{2,1,0:T(8,128)(2,1)S(1)}, u32[]{:S(2)}, u32[]{:S(2)}) collective-permute-start(bf16[2,128,256]{2,1,0:T(8,128)(2,1)S(1)} %pad_maximum_fusion.8.refs_0_), channel_id=1, source_target_pairs={{0,4},{1,5},{2,6},{3,7},{4,0},{5,1},{6,2},{7,3},{8,12},{9,13},{10,... | collective-permute-start | bytes 393224 | tf_op jit(solution)/shard_map/ppermute | solution.py:17
  95.9 2.2 %collective-permute-start.6 = (bf16[2,128,256]{2,1,0:T(8,128)(2,1)S(1)}, bf16[2,128,256]{2,1,0:T(8,128)(2,1)}, u32[]{:S(2)}, u32[]{:S(2)}) collective-permute-start(bf16[2,128,256]{2,1,0:T(8,128)(2,1)S(1)} %pad_maximum_fusion.8.refs_0_), channel_id=1, source_target_pairs={{0,7},{1,0},{2,1},{3,2},{4,3},{5,4},{6,5},{7,6},{8,15},{9,8},{10,9... | collective-permute-start | bytes 393224 | tf_op jit(solution)/shard_map/ppermute | solution.py:17
  98.1 3.1 %collective-permute-start.5 = (bf16[2,128,256]{2,1,0:T(8,128)(2,1)S(1)}, bf16[2,128,256]{2,1,0:T(8,128)(2,1)}, u32[]{:S(2)}, u32[]{:S(2)}) collective-permute-start(bf16[2,128,256]{2,1,0:T(8,128)(2,1)S(1)} %pad_maximum_fusion.8.refs_0_), channel_id=1, source_target_pairs={{0,1},{1,2},{2,3},{3,4},{4,5},{5,6},{6,7},{7,0},{8,9},{9,10},{10,1... | collective-permute-start | bytes 393224 | tf_op jit(solution)/shard_map/ppermute | solution.py:17
  101.2 2.2 %collective-permute-start.4 = (bf16[2,128,256]{2,1,0:T(8,128)(2,1)S(1)}, bf16[2,128,256]{2,1,0:T(8,128)(2,1)}, u32[]{:S(2)}, u32[]{:S(2)}) collective-permute-start(bf16[2,128,256]{2,1,0:T(8,128)(2,1)S(1)} %pad_maximum_fusion.8.refs_0_), channel_id=1, source_target_pairs={{0,6},{1,7},{2,0},{3,1},{4,2},{5,3},{6,4},{7,5},{8,14},{9,15},{10,... | collective-permute-start | bytes 393224 | tf_op jit(solution)/shard_map/ppermute | solution.py:17
  103.4 11.7 %collective-permute-done.7.refs_7_ = bf16[2,128,256]{2,1,0:T(8,128)(2,1)S(1)} collective-permute-done((bf16[2,128,256]{2,1,0:T(8,128)(2,1)S(1)}, bf16[2,128,256]{2,1,0:T(8,128)(2,1)S(1)}, u32[]{:S(2)}, u32[]{:S(2)}) %collective-permute-start.7) | collective-permute-done | bytes 131104 | tf_op jit(solution)/shard_map/ppermute | solution.py:17
  115.1 3.1 %collective-permute-start.9 = (bf16[8,16,4096]{2,1,0:T(8,128)(2,1)S(1)}, bf16[8,16,4096]{2,1,0:T(8,128)(2,1)}, u32[]{:S(2)}, u32[]{:S(2)}) collective-permute-start(bf16[8,16,4096]{2,1,0:T(8,128)(2,1)S(1)} %all-to-all-done.1), channel_id=1, source_target_pairs={{0,8},{8,0},{1,9},{9,1},{2,10},{10,2},{3,11},{11,3},{4,12},{12,4},... | collective-permute-start | bytes 3145736 | tf_op jit(solution)/shard_map/ppermute | solution.py:21
  118.2 1.9 %collective-permute-start.3 = (bf16[2,128,256]{2,1,0:T(8,128)(2,1)S(1)}, bf16[2,128,256]{2,1,0:T(8,128)(2,1)S(1)}, u32[]{:S(2)}, u32[]{:S(2)}) collective-permute-start(bf16[2,128,256]{2,1,0:T(8,128)(2,1)S(1)} %pad_maximum_fusion.8.refs_0_), channel_id=1, source_target_pairs={{0,2},{1,3},{2,4},{3,5},{4,6},{5,7},{6,0},{7,1},{8,10},{9,11},{10,... | collective-permute-start | bytes 393224 | tf_op jit(solution)/shard_map/ppermute | solution.py:17
  120.2 2.5 %collective-permute-start.2 = (bf16[2,128,256]{2,1,0:T(8,128)(2,1)S(1)}, bf16[2,128,256]{2,1,0:T(8,128)(2,1)S(1)}, u32[]{:S(2)}, u32[]{:S(2)}) collective-permute-start(bf16[2,128,256]{2,1,0:T(8,128)(2,1)S(1)} %pad_maximum_fusion.8.refs_0_), channel_id=1, source_target_pairs={{0,5},{1,6},{2,7},{3,0},{4,1},{5,2},{6,3},{7,4},{8,13},{9,14},{10,... | collective-permute-start | bytes 393224 | tf_op jit(solution)/shard_map/ppermute | solution.py:17
  122.7 4.6 %collective-permute-start.1 = (bf16[2,128,256]{2,1,0:T(8,128)(2,1)S(1)}, bf16[2,128,256]{2,1,0:T(8,128)(2,1)S(1)}, u32[]{:S(2)}, u32[]{:S(2)}) collective-permute-start(bf16[2,128,256]{2,1,0:T(8,128)(2,1)S(1)} %pad_maximum_fusion.8.refs_0_), channel_id=1, source_target_pairs={{0,3},{1,4},{2,5},{3,6},{4,7},{5,0},{6,1},{7,2},{8,11},{9,12},{10,... | collective-permute-start | bytes 393224 | tf_op jit(solution)/shard_map/ppermute | solution.py:17
  127.3 1.6 collective-permute-done.3.refs_3_
  128.8 3.2 %collective-permute-done.2.refs_2_ = bf16[2,128,256]{2,1,0:T(8,128)(2,1)S(1)} collective-permute-done((bf16[2,128,256]{2,1,0:T(8,128)(2,1)S(1)}, bf16[2,128,256]{2,1,0:T(8,128)(2,1)S(1)}, u32[]{:S(2)}, u32[]{:S(2)}) %collective-permute-start.2) | collective-permute-done | bytes 131104 | tf_op jit(solution)/shard_map/ppermute | solution.py:17
  132.0 0.8 collective-permute-done.1.refs_1_
  132.8 2.1 %join.1 = bf16[16,128,256]{2,1,0:T(8,128)(2,1)} custom-call(bf16[2,128,256]{2,1,0:T(8,128)(2,1)S(1)} %pad_maximum_fusion.8.refs_0_, bf16[2,128,256]{2,1,0:T(8,128)(2,1)S(1)} %collective-permute-done.1.refs_1_, bf16[2,128,256]{2,1,0:T(8,128)(2,1)S(1)} %collective-permute-done.2.refs_2_, bf16[2,128,256]{2,1,0:T(8,128)(2,1)S(1)} %collective-permute-done.3.refs_3_, ...), custom_call_target="tpu_custom_call" | custom-call | bytes 2097152 | tf_op jit(solution)/shard_map/join/pallas_call | solution.py:42
  134.9 8.3 %collective-permute-start.8 = (bf16[16,128,256]{2,1,0:T(8,128)(2,1)}, bf16[16,128,256]{2,1,0:T(8,128)(2,1)}, u32[]{:S(2)}, u32[]{:S(2)}) collective-permute-start(bf16[16,128,256]{2,1,0:T(8,128)(2,1)} %join.1), channel_id=1, source_target_pairs={{0,128},{128,0},{1,129},{129,1},{2,130},{130,2},{3,131},{131,3},{4... | collective-permute-start | bytes 3145736 | tf_op jit(solution)/shard_map/ppermute | solution.py:21
  143.2 6.2 %products.1 = bf16[256,1024]{1,0:T(8,128)(2,1)S(1)} custom-call(bf16[128,4096]{1,0:T(8,128)(2,1)S(1)} %bitcast.34, bf16[128,4096]{1,0:T(8,128)(2,1)} %bitcast.9.far_ref, bf16[1024,2048]{1,0:T(8,128)(2,1)} %weight_ref.1, bf16[512,2048]{1,0:T(8,128)(2,1)S(1)} %collective-permute-done.10.near_other_ref, bf16[512,2048]{1,0:T(8,128)(2,1)} %collective-permute-done.11.last_other_ref), custom_call_target="tpu_custom_call" | custom-call | flops 2147483648 | bytes 33554432 | tf_op jit(solution)/shard_map/products/pallas_call | solution.py:77
  149.5 0.8 copy-done.1
  150.2 3.5 %all-to-all-start.2 = ((bf16[8,32,1024]{2,1,0:T(8,128)(2,1)}), bf16[8,32,1024]{2,1,0:T(8,128)(2,1)S(1)}, u32[]{:S(2)}, u32[]{:S(2)}) async-start(bf16[8,32,1024]{2,1,0:T(8,128)(2,1)} %bitcast.35), calls=%async_computation.2 | async-start | bytes 1048576 | tf_op jit(solution)/shard_map/all_to_all | solution.py:29
  153.7 3.5 %fusion.4 = bf16[256,256]{1,0:T(8,128)(2,1)S(1)} fusion(bf16[16,128,256]{2,1,0:T(8,128)(2,1)} %collective-permute-done.8, bf16[16,128,256]{2,1,0:T(8,128)(2,1)} %join.1, bf16[1,1,256,256]{3,2,1,0:T(8,128)(2,1)S(1)} %copy-done), kind=kOutput, calls=%fused_computation.4 | convolution fusion | flops 1083179008 | bytes 2359296 | tf_op jit(solution)/shard_map/pad,pbd->ab/dot_general | solution.py:133
  157.3 0.7 fusion.11
  158.0 13.7 %all-to-all-done.2 = bf16[8,32,1024]{2,1,0:T(8,128)(2,1)S(1)} async-done(((bf16[8,32,1024]{2,1,0:T(8,128)(2,1)}), bf16[8,32,1024]{2,1,0:T(8,128)(2,1)S(1)}, u32[]{:S(2)}, u32[]{:S(2)}) %all-to-all-start.2) | async-done | bytes 524320 | tf_op jit(solution)/shard_map/all_to_all | solution.py:29
  171.8 0.7 copy.12
  (27 shorter events, 1.0 us)
Async XLA Ops:
  0.6 7.4 %copy-start = (bf16[1,1,256,256]{3,2,1,0:T(8,128)(2,1)S(1)}, bf16[1,1,256,256]{3,2,1,0:T(8,128)(2,1)}, u32[]{:S(2)}) copy-start(bf16[1,1,256,256]{3,2,1,0:T(8,128)(2,1)} %param.4) | copy-start | bytes 393220
  0.7 7.4 %copy-start.3 = (s32[256]{0:T(256)S(1)}, s32[256]{0:T(256)}, u32[]{:S(2)}) copy-start(s32[256]{0:T(256)} %param.7) | copy-start | bytes 3076
  3.9 76.3 %collective-permute-start.10 = (bf16[512,2048]{1,0:T(8,128)(2,1)}, bf16[512,2048]{1,0:T(8,128)(2,1)S(1)}, u32[]{:S(2)}, u32[]{:S(2)}) collective-permute-start(bf16[512,2048]{1,0:T(8,128)(2,1)} %constant_dynamic-slice_fusion), channel_id=1, source_target_pairs={{0,16},{16,0},{1,17},{17,1},{2,18},{18,2},{3,19},{19,3},{4,20},{20... | collective-permute-start | bytes 6291464 | tf_op jit(solution)/shard_map/ppermute | solution.py:21
  9.3 52.8 %all-to-all-start = ((bf16[64,8,128]{2,1,0:T(8,128)(2,1)}), bf16[64,8,128]{2,1,0:T(8,128)(2,1)S(1)}, u32[]{:S(2)}, u32[]{:S(2)}) async-start(bf16[64,8,128]{2,1,0:T(8,128)(2,1)} %reshape.46), calls=%async_computation | async-start | bytes 262144 | tf_op jit(solution)/shard_map/all_to_all | solution.py:29
  62.3 20.5 %copy-start.2 = (bf16[1,256,256]{2,1,0:T(8,128)(2,1)S(1)}, bf16[1,256,256]{2,1,0:T(8,128)(2,1)}, u32[]{:S(2)}) copy-start(bf16[1,256,256]{2,1,0:T(8,128)(2,1)} %param.5) | copy-start | bytes 393220
  63.8 51.3 %all-to-all-start.1 = ((bf16[8,16,4096]{2,1,0:T(8,128)(2,1)}), bf16[8,16,4096]{2,1,0:T(8,128)(2,1)S(1)}, u32[]{:S(2)}, u32[]{:S(2)}) async-start(bf16[8,16,4096]{2,1,0:T(8,128)(2,1)} %broadcast_in_dim.2), calls=%async_computation.1 | async-start | bytes 2097152 | tf_op jit(solution)/shard_map/all_to_all | solution.py:29
  80.2 63.0 %collective-permute-start.11 = (bf16[512,2048]{1,0:T(8,128)(2,1)S(1)}, bf16[512,2048]{1,0:T(8,128)(2,1)}, u32[]{:S(2)}, u32[]{:S(2)}) collective-permute-start(bf16[512,2048]{1,0:T(8,128)(2,1)S(1)} %collective-permute-done.10.near_other_ref), channel_id=1, source_target_pairs={{0,128},{128,0},{1,129},{129,1},{2,130},{130,2},{3,131},{131,3},{4... | collective-permute-start | bytes 6291464 | tf_op jit(solution)/shard_map/ppermute | solution.py:21
  82.8 5.5 %collective-permute-start = (bf16[1,128,256]{2,1,0:T(8,128)(2,1)S(1)}, bf16[1,128,256]{2,1,0:T(8,128)(2,1)S(1)}, u32[]{:S(2)}, u32[]{:S(2)}) collective-permute-start(bf16[1,128,256]{2,1,0:T(8,128)(2,1)S(1)} %constant_dynamic-slice_fusion.1), channel_id=1, source_target_pairs={{0,8},{8,0},{1,9},{9,1},{2,10},{10,2},{3,11},{11,3},{4,12},{12,4},... | collective-permute-start | bytes 196616 | tf_op jit(solution)/shard_map/ppermute | solution.py:21
  88.4 26.7 %collective-permute-start.7 = (bf16[2,128,256]{2,1,0:T(8,128)(2,1)S(1)}, bf16[2,128,256]{2,1,0:T(8,128)(2,1)S(1)}, u32[]{:S(2)}, u32[]{:S(2)}) collective-permute-start(bf16[2,128,256]{2,1,0:T(8,128)(2,1)S(1)} %pad_maximum_fusion.8.refs_0_), channel_id=1, source_target_pairs={{0,4},{1,5},{2,6},{3,7},{4,0},{5,1},{6,2},{7,3},{8,12},{9,13},{10,... | collective-permute-start | bytes 393224 | tf_op jit(solution)/shard_map/ppermute | solution.py:17
  95.9 22.3 %collective-permute-start.6 = (bf16[2,128,256]{2,1,0:T(8,128)(2,1)S(1)}, bf16[2,128,256]{2,1,0:T(8,128)(2,1)}, u32[]{:S(2)}, u32[]{:S(2)}) collective-permute-start(bf16[2,128,256]{2,1,0:T(8,128)(2,1)S(1)} %pad_maximum_fusion.8.refs_0_), channel_id=1, source_target_pairs={{0,7},{1,0},{2,1},{3,2},{4,3},{5,4},{6,5},{7,6},{8,15},{9,8},{10,9... | collective-permute-start | bytes 393224 | tf_op jit(solution)/shard_map/ppermute | solution.py:17
  98.1 22.0 %collective-permute-start.5 = (bf16[2,128,256]{2,1,0:T(8,128)(2,1)S(1)}, bf16[2,128,256]{2,1,0:T(8,128)(2,1)}, u32[]{:S(2)}, u32[]{:S(2)}) collective-permute-start(bf16[2,128,256]{2,1,0:T(8,128)(2,1)S(1)} %pad_maximum_fusion.8.refs_0_), channel_id=1, source_target_pairs={{0,1},{1,2},{2,3},{3,4},{4,5},{5,6},{6,7},{7,0},{8,9},{9,10},{10,1... | collective-permute-start | bytes 393224 | tf_op jit(solution)/shard_map/ppermute | solution.py:17
  101.2 21.5 %collective-permute-start.4 = (bf16[2,128,256]{2,1,0:T(8,128)(2,1)S(1)}, bf16[2,128,256]{2,1,0:T(8,128)(2,1)}, u32[]{:S(2)}, u32[]{:S(2)}) collective-permute-start(bf16[2,128,256]{2,1,0:T(8,128)(2,1)S(1)} %pad_maximum_fusion.8.refs_0_), channel_id=1, source_target_pairs={{0,6},{1,7},{2,0},{3,1},{4,2},{5,3},{6,4},{7,5},{8,14},{9,15},{10,... | collective-permute-start | bytes 393224 | tf_op jit(solution)/shard_map/ppermute | solution.py:17
  115.1 28.1 %collective-permute-start.9 = (bf16[8,16,4096]{2,1,0:T(8,128)(2,1)S(1)}, bf16[8,16,4096]{2,1,0:T(8,128)(2,1)}, u32[]{:S(2)}, u32[]{:S(2)}) collective-permute-start(bf16[8,16,4096]{2,1,0:T(8,128)(2,1)S(1)} %all-to-all-done.1), channel_id=1, source_target_pairs={{0,8},{8,0},{1,9},{9,1},{2,10},{10,2},{3,11},{11,3},{4,12},{12,4},... | collective-permute-start | bytes 3145736 | tf_op jit(solution)/shard_map/ppermute | solution.py:21
  118.2 10.6 %collective-permute-start.3 = (bf16[2,128,256]{2,1,0:T(8,128)(2,1)S(1)}, bf16[2,128,256]{2,1,0:T(8,128)(2,1)S(1)}, u32[]{:S(2)}, u32[]{:S(2)}) collective-permute-start(bf16[2,128,256]{2,1,0:T(8,128)(2,1)S(1)} %pad_maximum_fusion.8.refs_0_), channel_id=1, source_target_pairs={{0,2},{1,3},{2,4},{3,5},{4,6},{5,7},{6,0},{7,1},{8,10},{9,11},{10,... | collective-permute-start | bytes 393224 | tf_op jit(solution)/shard_map/ppermute | solution.py:17
  120.2 11.8 %collective-permute-start.2 = (bf16[2,128,256]{2,1,0:T(8,128)(2,1)S(1)}, bf16[2,128,256]{2,1,0:T(8,128)(2,1)S(1)}, u32[]{:S(2)}, u32[]{:S(2)}) collective-permute-start(bf16[2,128,256]{2,1,0:T(8,128)(2,1)S(1)} %pad_maximum_fusion.8.refs_0_), channel_id=1, source_target_pairs={{0,5},{1,6},{2,7},{3,0},{4,1},{5,2},{6,3},{7,4},{8,13},{9,14},{10,... | collective-permute-start | bytes 393224 | tf_op jit(solution)/shard_map/ppermute | solution.py:17
  122.7 10.1 %collective-permute-start.1 = (bf16[2,128,256]{2,1,0:T(8,128)(2,1)S(1)}, bf16[2,128,256]{2,1,0:T(8,128)(2,1)S(1)}, u32[]{:S(2)}, u32[]{:S(2)}) collective-permute-start(bf16[2,128,256]{2,1,0:T(8,128)(2,1)S(1)} %pad_maximum_fusion.8.refs_0_), channel_id=1, source_target_pairs={{0,3},{1,4},{2,5},{3,6},{4,7},{5,0},{6,1},{7,2},{8,11},{9,12},{10,... | collective-permute-start | bytes 393224 | tf_op jit(solution)/shard_map/ppermute | solution.py:17
  134.9 18.8 %collective-permute-start.8 = (bf16[16,128,256]{2,1,0:T(8,128)(2,1)}, bf16[16,128,256]{2,1,0:T(8,128)(2,1)}, u32[]{:S(2)}, u32[]{:S(2)}) collective-permute-start(bf16[16,128,256]{2,1,0:T(8,128)(2,1)} %join.1), channel_id=1, source_target_pairs={{0,128},{128,0},{1,129},{129,1},{2,130},{130,2},{3,131},{131,3},{4... | collective-permute-start | bytes 3145736 | tf_op jit(solution)/shard_map/ppermute | solution.py:21
  149.5 0.8 copy-start.1
  150.2 21.5 %all-to-all-start.2 = ((bf16[8,32,1024]{2,1,0:T(8,128)(2,1)}), bf16[8,32,1024]{2,1,0:T(8,128)(2,1)S(1)}, u32[]{:S(2)}, u32[]{:S(2)}) async-start(bf16[8,32,1024]{2,1,0:T(8,128)(2,1)} %bitcast.35), calls=%async_computation.2 | async-start | bytes 1048576 | tf_op jit(solution)/shard_map/all_to_all | solution.py:29

commit v2 on v1

v2 whole, which is shorter than its diff:
```python
import jax
import jax.numpy as jnp
from jax import lax
from jax.experimental import pallas as pl
from jax.experimental.pallas import tpu as pltpu
from jax.sharding import Mesh, PartitionSpec as P

VMEM = 20 * 1024 * 1024
PRODUCT_VMEM = 52 * 1024 * 1024
AXES = ("hi", "core", "row", "lo", "z")


def shift(x, by):
    depth = lax.axis_size("z")
    return lax.ppermute(x, "z", [(i, (i + by) % depth) for i in range(depth)])


def swap(x, axis):
    return lax.ppermute(x, axis, [(0, 1), (1, 0)])


def exchange(x, axes):
    return lax.all_to_all(x, axes, 0, 0, tiled=True)


def join_kernel(*refs):
    pieces, out_ref = refs[:-1], refs[-1]
    at = 0
    for piece in pieces:
        out_ref[pl.ds(at, piece.shape[0])] = piece[...]
        at += piece.shape[0]


def joined(blocks):
    shape = (sum(b.shape[0] for b in blocks), *blocks[0].shape[1:])
    size = 4 * sum(b.size for b in blocks)
    return pl.pallas_call(
        join_kernel,
        in_specs=[pl.BlockSpec(memory_space=pltpu.VMEM)] * len(blocks),
        out_specs=pl.BlockSpec(memory_space=pltpu.VMEM),
        out_shape=jax.ShapeDtypeStruct(shape, blocks[0].dtype),
        cost_estimate=pl.CostEstimate(flops=0, bytes_accessed=size, transcendentals=0),
        compiler_params=pltpu.CompilerParams(vmem_limit_bytes=VMEM),
        name="join",
    )(*blocks)


def product_kernel(near_ref, far_ref, weight_ref, out_ref, held, sems):
    low = lax.axis_index("lo")
    count = near_ref.shape[0]
    steps, tile, _ = held.shape
    copies = [pltpu.make_async_copy(weight_ref.at[pl.ds(i * tile, tile)], held.at[i], sems.at[i]) for i in range(steps)]
    for copy in copies:
        copy.start()
    panel = jnp.concatenate([near_ref[...], far_ref[...]], axis=0)
    for i in range(steps):
        copies[i].wait()
        sums = lax.dot_general(held[i], panel, (((1,), (1,)), ((), ())), preferred_element_type=jnp.float32)
        sums = sums.T.astype(out_ref.dtype)
        columns = pl.ds(i * tile, tile)
        out_ref[pl.ds(pl.multiple_of(low * count, count), count), columns] = sums[:count]
        out_ref[pl.ds(pl.multiple_of((1 - low) * count, count), count), columns] = sums[count:]


def products(near, far, weight):
    count, outs = near.shape[0], weight.shape[0]
    steps = 4
    return pl.pallas_call(
        product_kernel,
        in_specs=[pl.BlockSpec(memory_space=pl.ANY if i == 2 else pltpu.VMEM) for i in range(3)],
        out_specs=pl.BlockSpec(memory_space=pltpu.VMEM),
        out_shape=jax.ShapeDtypeStruct((2 * count, outs), jnp.bfloat16),
        scratch_shapes=[
            pltpu.VMEM((steps, outs // steps, weight.shape[1]), jnp.bfloat16),
            pltpu.SemaphoreType.DMA((steps,)),
        ],
        cost_estimate=pl.CostEstimate(
            flops=4 * near.size * outs, bytes_accessed=2 * weight.size + 8 * near.size, transcendentals=0
        ),
        compiler_params=pltpu.CompilerParams(vmem_limit_bytes=PRODUCT_VMEM),
        name="products",
    )(near, far, weight)


def body(amplitudes, factors, cycle_weight, orbital_order):
    virtual = amplitudes.shape[2]
    pair = amplitudes.reshape(virtual, virtual)
    groups = lax.axis_size("hi") * lax.axis_size("core")
    rows = lax.axis_size("row")
    depth = lax.axis_size("z")
    width = virtual // groups
    block = virtual // rows
    outs, inner = cycle_weight.shape
    core = lax.axis_index("core")

    half = virtual // 2
    mine = lax.dynamic_slice_in_dim(factors, core * half, half, axis=1)
    both = jnp.concatenate([mine, swap(mine, "lo")])

    pick = (orbital_order[:, None] == jnp.arange(virtual, dtype=jnp.int32)[None, :]).astype(jnp.bfloat16)
    ordered = jnp.einsum("xd,cd->xc", pick, pair, preferred_element_type=jnp.float32).astype(jnp.bfloat16)
    tiles = ordered.reshape(groups, width, rows, block)
    tiles = jnp.transpose(tiles, (0, 2, 1, 3)).reshape(groups * rows, width * block // 128, 128)
    arrived = exchange(tiles, ("hi", "core", "row"))
    own = arrived.reshape(groups * rows, width, block)
    own = jnp.transpose(own, (1, 2, 0)).reshape(width, inner)

    chunk = width // 2

    def gathered(part):
        copies = jnp.broadcast_to(part, (depth, *part.shape))
        return exchange(copies, "z").reshape(depth * chunk, inner)

    near_a = gathered(own[:chunk])
    near_b = gathered(own[chunk:])
    far_a = swap(near_a, "lo")
    far_b = swap(near_b, "lo")

    left = shift(both, 1)
    right = shift(both, -1)
    left_two = shift(jnp.concatenate([both, left]), 2)
    right_two = shift(jnp.concatenate([both, right]), -2)
    opposite = shift(both, depth // 2)

    def summed(near, far):
        parts = products(near, far, cycle_weight).reshape(rows, -1, outs)
        parts = exchange(parts, "row")
        total = jnp.sum(parts.astype(jnp.float32), axis=0).astype(jnp.bfloat16)
        return total.reshape(-1, chunk, outs)

    total_a = summed(near_a, far_a)
    total_b = summed(near_b, far_b)
    cycle_term = jnp.concatenate([total_a, total_b], axis=1).reshape(-1, outs)

    halves = joined([both, left, right, left_two, right_two, opposite])
    others = swap(halves, "core")
    whole = jnp.concatenate([halves, others], axis=1)
    dressed = jnp.einsum("pac,cd->pad", whole, pair, preferred_element_type=jnp.float32).astype(jnp.bfloat16)
    ladder = jnp.einsum("pad,pbd->ab", dressed, whole, preferred_element_type=jnp.float32)
    swapped = jnp.roll(ladder, (half, half), (0, 1))
    ladder_term = jnp.where(core == 0, ladder, swapped).astype(jnp.bfloat16).reshape(amplitudes.shape)
    return (ladder_term, cycle_term)


def solution(mesh):
    groups, rows, cols = mesh.devices.shape
    split = Mesh(mesh.devices.reshape(groups // 2, 2, rows, 2, cols // 2), AXES)
    row, col = "row", ("lo", "z")
    pairs = P(("hi", "core", row), col, None, None)
    return jax.shard_map(
        body,
        mesh=split,
        in_specs=(pairs, P(col, None, None), P(col, row), P()),
        out_specs=(pairs, P(("hi", "core", row), col)),
        check_vma=False,
    )
```

time: 173 us -> 169 us (0.977)
  the two profiles are of different devices: /device:TPU:1 before, /device:TPU:128 now
where the time goes in v2:
time: 169 us; the launch traced here: 168 us
  starting transfers between devices  62.1 us (37%)
  waiting for transfers between devices  59.4 us (35%)
  blocking collectives  26.2 us (16%)
  Pallas kernels  10.6 us (6%)
  matrix products  3.89 us (2%)
  local copies, waits for them, and re-layouts  3.83 us (2%)
    all_to_all x4, starting transfers between devices, exchange(): return lax.all_to_all(x, axes, 0, 0, tiled=True)  32.4 us
    all_to_all x4, waiting for transfers between devices, exchange(): return lax.all_to_all(x, axes, 0, 0, tiled=True)  28.2 us
    all_to_all x1, blocking collectives, exchange(): return lax.all_to_all(x, axes, 0, 0, tiled=True)  26.2 us
    ppermute x5, starting transfers between devices, shift(): return lax.ppermute(x, 'z', [(i, (i + by) % depth) for i in range(depth)])  19.6 us
    ppermute x4, waiting for transfers between devices, swap(): return lax.ppermute(x, axis, [(0, 1), (1, 0)])  16.5 us
    ppermute x5, waiting for transfers between devices, shift(): return lax.ppermute(x, 'z', [(i, (i + by) % depth) for i in range(depth)])  14.7 us
    pallas_call x2, Pallas kernels, products(): pl.pallas_call(product_kernel, in_specs=[pl.BlockSpec(memory_space=pl.ANY...  10.5 us
    ppermute x4, starting transfers between devices, swap(): return lax.ppermute(x, axis, [(0, 1), (1, 0)])  10.1 us
  transfers between devices with their start and end apart: 13, of which 6 were waited for; matrix products, arithmetic and copies ran while one was open for 2% of the time, Pallas kernels for 6%

profile of v2, /device:TPU:128, one launch (start us, length us, event | category | flops | bytes accessed | tf_op | source)
XLA Modules:
  0.0 168.5 jit_solution(638310179293310113)
XLA Ops:
  0.6 0.9 copy-done
  1.5 0.9 convolution_convert_fusion
  2.5 0.2 reshape.46
  2.8 0.3 reshape.47
  3.1 26.2 %all_to_all.25 = bf16[64,8,128]{2,1,0:T(8,128)(2,1)S(1)} all-to-all(bf16[64,8,128]{2,1,0:T(8,128)(2,1)S(1)} %reshape.47), channel_id=1, replica_groups=mesh['hi'=4,'core'=2,'row'=8,'lo'=2,'z'=8] {'hi','core','row'}, dimensions={0} | all-to-all | bytes 262144 | tf_op jit(solution)/shard_map/all_to_all | solution.py:23
  29.3 0.2 copy.8
  29.7 0.8 broadcast_in_dim.9
  30.6 15.4 %all-to-all-start.3 = ((bf16[8,16,2048]{2,1,0:T(8,128)(2,1)}), bf16[8,16,2048]{2,1,0:T(8,128)(2,1)S(1)}, u32[]{:S(2)}, u32[]{:S(2)}) async-start(bf16[8,16,2048]{2,1,0:T(8,128)(2,1)} %broadcast_in_dim.9), calls=%async_computation.3 | async-start | bytes 1048576 | tf_op jit(solution)/shard_map/all_to_all | solution.py:23
  46.2 15.2 %all-to-all-done.3 = bf16[8,16,2048]{2,1,0:T(8,128)(2,1)S(1)} async-done(((bf16[8,16,2048]{2,1,0:T(8,128)(2,1)}), bf16[8,16,2048]{2,1,0:T(8,128)(2,1)S(1)}, u32[]{:S(2)}, u32[]{:S(2)}) %all-to-all-start.3) | async-done | bytes 524320 | tf_op jit(solution)/shard_map/all_to_all | solution.py:23
  61.4 0.9 broadcast_in_dim.8
  62.3 4.9 %all-to-all-start.1 = ((bf16[8,16,2048]{2,1,0:T(8,128)(2,1)}), bf16[8,16,2048]{2,1,0:T(8,128)(2,1)S(1)}, u32[]{:S(2)}, u32[]{:S(2)}) async-start(bf16[8,16,2048]{2,1,0:T(8,128)(2,1)} %broadcast_in_dim.8), calls=%async_computation.1 | async-start | bytes 1048576 | tf_op jit(solution)/shard_map/all_to_all | solution.py:23
  67.1 2.6 %collective-permute-start = (bf16[1,128,256]{2,1,0:T(8,128)(2,1)S(1)}, bf16[1,128,256]{2,1,0:T(8,128)(2,1)S(1)}, u32[]{:S(2)}, u32[]{:S(2)}) collective-permute-start(bf16[1,128,256]{2,1,0:T(8,128)(2,1)S(1)} %constant_dynamic-slice_fusion), channel_id=1, source_target_pairs={{0,8},{8,0},{1,9},{9,1},{2,10},{10,2},{3,11},{11,3},{4,12},{12,4},... | collective-permute-start | bytes 196616 | tf_op jit(solution)/shard_map/ppermute | solution.py:19
  69.7 3.6 %collective-permute-done = bf16[1,128,256]{2,1,0:T(8,128)(2,1)S(1)} collective-permute-done((bf16[1,128,256]{2,1,0:T(8,128)(2,1)S(1)}, bf16[1,128,256]{2,1,0:T(8,128)(2,1)S(1)}, u32[]{:S(2)}, u32[]{:S(2)}) %collective-permute-start) | collective-permute-done | bytes 65568 | tf_op jit(solution)/shard_map/ppermute | solution.py:19
  73.3 3.4 %collective-permute-start.1 = (bf16[2,128,256]{2,1,0:T(8,128)(2,1)S(1)}, bf16[2,128,256]{2,1,0:T(8,128)(2,1)S(1)}, u32[]{:S(2)}, u32[]{:S(2)}) collective-permute-start(bf16[2,128,256]{2,1,0:T(8,128)(2,1)S(1)} %pad_maximum_fusion.11.refs_0_), channel_id=1, source_target_pairs={{0,1},{1,2},{2,3},{3,4},{4,5},{5,6},{6,7},{7,0},{8,9},{9,10},{10,1... | collective-permute-start | bytes 393224 | tf_op jit(solution)/shard_map/ppermute | solution.py:15
  76.7 2.5 %collective-permute-start.2 = (bf16[2,128,256]{2,1,0:T(8,128)(2,1)S(1)}, bf16[2,128,256]{2,1,0:T(8,128)(2,1)S(1)}, u32[]{:S(2)}, u32[]{:S(2)}) collective-permute-start(bf16[2,128,256]{2,1,0:T(8,128)(2,1)S(1)} %pad_maximum_fusion.11.refs_0_), channel_id=1, source_target_pairs={{0,7},{1,0},{2,1},{3,2},{4,3},{5,4},{6,5},{7,6},{8,15},{9,8},{10,9... | collective-permute-start | bytes 393224 | tf_op jit(solution)/shard_map/ppermute | solution.py:15
  79.2 2.6 %collective-permute-start.8 = (bf16[128,2048]{1,0:T(8,128)(2,1)S(1)}, bf16[128,2048]{1,0:T(8,128)(2,1)S(1)}, u32[]{:S(2)}, u32[]{:S(2)}) collective-permute-start(bf16[128,2048]{1,0:T(8,128)(2,1)S(1)} %bitcast.27), channel_id=1, source_target_pairs={{0,8},{8,0},{1,9},{9,1},{2,10},{10,2},{3,11},{11,3},{4,12},{12,4},... | collective-permute-start | bytes 1572872 | tf_op jit(solution)/shard_map/ppermute | solution.py:19
  81.8 2.1 %collective-permute-done.2.refs_2_ = bf16[2,128,256]{2,1,0:T(8,128)(2,1)S(1)} collective-permute-done((bf16[2,128,256]{2,1,0:T(8,128)(2,1)S(1)}, bf16[2,128,256]{2,1,0:T(8,128)(2,1)S(1)}, u32[]{:S(2)}, u32[]{:S(2)}) %collective-permute-start.2) | collective-permute-done | bytes 131104 | tf_op jit(solution)/shard_map/ppermute | solution.py:15
  83.9 6.4 %collective-permute-start.3 = (bf16[4,128,256]{2,1,0:T(8,128)(2,1)S(1)}, bf16[4,128,256]{2,1,0:T(8,128)(2,1)S(1)}, u32[]{:S(2)}, u32[]{:S(2)}) collective-permute-start(bf16[4,128,256]{2,1,0:T(8,128)(2,1)S(1)} %get-tuple-element.7), channel_id=1, source_target_pairs={{0,2},{1,3},{2,4},{3,5},{4,6},{5,7},{6,0},{7,1},{8,10},{9,11},{10,... | collective-permute-start | bytes 786440 | tf_op jit(solution)/shard_map/ppermute | solution.py:15
  90.3 1.9 %collective-permute-start.4 = (bf16[4,128,256]{2,1,0:T(8,128)(2,1)S(1)}, bf16[4,128,256]{2,1,0:T(8,128)(2,1)S(1)}, u32[]{:S(2)}, u32[]{:S(2)}) collective-permute-start(bf16[4,128,256]{2,1,0:T(8,128)(2,1)S(1)} %get-tuple-element.6), channel_id=1, source_target_pairs={{0,6},{1,7},{2,0},{3,1},{4,2},{5,3},{6,4},{7,5},{8,14},{9,15},{10,... | collective-permute-start | bytes 786440 | tf_op jit(solution)/shard_map/ppermute | solution.py:15
  92.2 5.5 %collective-permute-start.5 = (bf16[2,128,256]{2,1,0:T(8,128)(2,1)S(1)}, bf16[2,128,256]{2,1,0:T(8,128)(2,1)S(1)}, u32[]{:S(2)}, u32[]{:S(2)}) collective-permute-start(bf16[2,128,256]{2,1,0:T(8,128)(2,1)S(1)} %pad_maximum_fusion.11.refs_0_), channel_id=1, source_target_pairs={{0,4},{1,5},{2,6},{3,7},{4,0},{5,1},{6,2},{7,3},{8,12},{9,13},{10,... | collective-permute-start | bytes 393224 | tf_op jit(solution)/shard_map/ppermute | solution.py:15
  97.7 12.6 %collective-permute-done.5.refs_5_ = bf16[2,128,256]{2,1,0:T(8,128)(2,1)S(1)} collective-permute-done((bf16[2,128,256]{2,1,0:T(8,128)(2,1)S(1)}, bf16[2,128,256]{2,1,0:T(8,128)(2,1)S(1)}, u32[]{:S(2)}, u32[]{:S(2)}) %collective-permute-start.5) | collective-permute-done | bytes 131104 | tf_op jit(solution)/shard_map/ppermute | solution.py:15
  110.4 1.9 %collective-permute-start.6 = (bf16[16,128,256]{2,1,0:T(8,128)(2,1)S(1)}, bf16[16,128,256]{2,1,0:T(8,128)(2,1)}, u32[]{:S(2)}, u32[]{:S(2)}) collective-permute-start(bf16[16,128,256]{2,1,0:T(8,128)(2,1)S(1)} %join.1), channel_id=1, source_target_pairs={{0,128},{128,0},{1,129},{129,1},{2,130},{130,2},{3,131},{131,3},{4... | collective-permute-start | bytes 3145736 | tf_op jit(solution)/shard_map/ppermute | solution.py:19
  112.3 5.3 %products.3 = bf16[256,1024]{1,0:T(8,128)(2,1)} custom-call(bf16[128,2048]{1,0:T(8,128)(2,1)S(1)} %bitcast.28, bf16[128,2048]{1,0:T(8,128)(2,1)S(1)} %collective-permute-done.8.far_ref, bf16[1024,2048]{1,0:T(8,128)(2,1)} %weight_ref.3), custom_call_target="tpu_custom_call" | custom-call | flops 1073741824 | bytes 6291456 | tf_op jit(solution)/shard_map/products/pallas_call | solution.py:68
  117.6 5.2 %all-to-all-start.4 = ((bf16[8,32,1024]{2,1,0:T(8,128)(2,1)}), bf16[8,32,1024]{2,1,0:T(8,128)(2,1)S(1)}, u32[]{:S(2)}, u32[]{:S(2)}) async-start(bf16[8,32,1024]{2,1,0:T(8,128)(2,1)} %bitcast.12), calls=%async_computation.4 | async-start | bytes 1048576 | tf_op jit(solution)/shard_map/all_to_all | solution.py:23
  122.8 3.0 %collective-permute-start.7 = (bf16[128,2048]{1,0:T(8,128)(2,1)S(1)}, bf16[128,2048]{1,0:T(8,128)(2,1)S(1)}, u32[]{:S(2)}, u32[]{:S(2)}) collective-permute-start(bf16[128,2048]{1,0:T(8,128)(2,1)S(1)} %bitcast.29), channel_id=1, source_target_pairs={{0,8},{8,0},{1,9},{9,1},{2,10},{10,2},{3,11},{11,3},{4,12},{12,4},... | collective-permute-start | bytes 1572872 | tf_op jit(solution)/shard_map/ppermute | solution.py:19
  125.8 13.0 %collective-permute-done.7.far_ref = bf16[128,2048]{1,0:T(8,128)(2,1)S(1)} collective-permute-done((bf16[128,2048]{1,0:T(8,128)(2,1)S(1)}, bf16[128,2048]{1,0:T(8,128)(2,1)S(1)}, u32[]{:S(2)}, u32[]{:S(2)}) %collective-permute-start.7) | collective-permute-done | bytes 524320 | tf_op jit(solution)/shard_map/ppermute | solution.py:19
  138.8 5.3 %products.2 = bf16[256,1024]{1,0:T(8,128)(2,1)} custom-call(bf16[128,2048]{1,0:T(8,128)(2,1)S(1)} %bitcast.30, bf16[128,2048]{1,0:T(8,128)(2,1)S(1)} %collective-permute-done.7.far_ref, bf16[1024,2048]{1,0:T(8,128)(2,1)} %weight_ref.3), custom_call_target="tpu_custom_call" | custom-call | flops 1073741824 | bytes 6291456 | tf_op jit(solution)/shard_map/products/pallas_call | solution.py:68
  144.0 6.9 %all-to-all-start.2 = ((bf16[8,32,1024]{2,1,0:T(8,128)(2,1)}), bf16[8,32,1024]{2,1,0:T(8,128)(2,1)S(1)}, u32[]{:S(2)}, u32[]{:S(2)}) async-start(bf16[8,32,1024]{2,1,0:T(8,128)(2,1)} %bitcast.8), calls=%async_computation.2 | async-start | bytes 1048576 | tf_op jit(solution)/shard_map/all_to_all | solution.py:23
  151.0 3.0 %fusion.4 = bf16[256,256]{1,0:T(8,128)(2,1)S(1)} fusion(bf16[16,128,256]{2,1,0:T(8,128)(2,1)} %collective-permute-done.6, bf16[16,128,256]{2,1,0:T(8,128)(2,1)S(1)} %join.1, bf16[1,1,256,256]{3,2,1,0:T(8,128)(2,1)S(1)} %copy-done), kind=kOutput, calls=%fused_computation.4 | convolution fusion | flops 1083179008 | bytes 2359296 | tf_op jit(solution)/shard_map/pad,pbd->ab/dot_general | solution.py:139
  154.0 0.7 fusion.11
  154.8 12.9 %all-to-all-done.2 = bf16[8,32,1024]{2,1,0:T(8,128)(2,1)S(1)} async-done(((bf16[8,32,1024]{2,1,0:T(8,128)(2,1)}), bf16[8,32,1024]{2,1,0:T(8,128)(2,1)S(1)}, u32[]{:S(2)}, u32[]{:S(2)}) %all-to-all-start.2) | async-done | bytes 524320 | tf_op jit(solution)/shard_map/all_to_all | solution.py:23
  167.8 0.7 pad_maximum_fusion.12
  (22 shorter events, 0.8 us)
Async XLA Ops:
  0.6 0.9 copy-start
  29.5 37.6 %copy-start.1 = (bf16[1,256,256]{2,1,0:T(8,128)(2,1)S(1)}, bf16[1,256,256]{2,1,0:T(8,128)(2,1)}, u32[]{:S(2)}) copy-start(bf16[1,256,256]{2,1,0:T(8,128)(2,1)} %param.5) | copy-start | bytes 393220
  30.6 30.8 %all-to-all-start.3 = ((bf16[8,16,2048]{2,1,0:T(8,128)(2,1)}), bf16[8,16,2048]{2,1,0:T(8,128)(2,1)S(1)}, u32[]{:S(2)}, u32[]{:S(2)}) async-start(bf16[8,16,2048]{2,1,0:T(8,128)(2,1)} %broadcast_in_dim.9), calls=%async_computation.3 | async-start | bytes 1048576 | tf_op jit(solution)/shard_map/all_to_all | solution.py:23
  62.3 55.4 %all-to-all-start.1 = ((bf16[8,16,2048]{2,1,0:T(8,128)(2,1)}), bf16[8,16,2048]{2,1,0:T(8,128)(2,1)S(1)}, u32[]{:S(2)}, u32[]{:S(2)}) async-start(bf16[8,16,2048]{2,1,0:T(8,128)(2,1)} %broadcast_in_dim.8), calls=%async_computation.1 | async-start | bytes 1048576 | tf_op jit(solution)/shard_map/all_to_all | solution.py:23
  67.1 6.2 %collective-permute-start = (bf16[1,128,256]{2,1,0:T(8,128)(2,1)S(1)}, bf16[1,128,256]{2,1,0:T(8,128)(2,1)S(1)}, u32[]{:S(2)}, u32[]{:S(2)}) collective-permute-start(bf16[1,128,256]{2,1,0:T(8,128)(2,1)S(1)} %constant_dynamic-slice_fusion), channel_id=1, source_target_pairs={{0,8},{8,0},{1,9},{9,1},{2,10},{10,2},{3,11},{11,3},{4,12},{12,4},... | collective-permute-start | bytes 196616 | tf_op jit(solution)/shard_map/ppermute | solution.py:19
  73.3 8.5 %collective-permute-start.1 = (bf16[2,128,256]{2,1,0:T(8,128)(2,1)S(1)}, bf16[2,128,256]{2,1,0:T(8,128)(2,1)S(1)}, u32[]{:S(2)}, u32[]{:S(2)}) collective-permute-start(bf16[2,128,256]{2,1,0:T(8,128)(2,1)S(1)} %pad_maximum_fusion.11.refs_0_), channel_id=1, source_target_pairs={{0,1},{1,2},{2,3},{3,4},{4,5},{5,6},{6,7},{7,0},{8,9},{9,10},{10,1... | collective-permute-start | bytes 393224 | tf_op jit(solution)/shard_map/ppermute | solution.py:15
  76.7 7.2 %collective-permute-start.2 = (bf16[2,128,256]{2,1,0:T(8,128)(2,1)S(1)}, bf16[2,128,256]{2,1,0:T(8,128)(2,1)S(1)}, u32[]{:S(2)}, u32[]{:S(2)}) collective-permute-start(bf16[2,128,256]{2,1,0:T(8,128)(2,1)S(1)} %pad_maximum_fusion.11.refs_0_), channel_id=1, source_target_pairs={{0,7},{1,0},{2,1},{3,2},{4,3},{5,4},{6,5},{7,6},{8,15},{9,8},{10,9... | collective-permute-start | bytes 393224 | tf_op jit(solution)/shard_map/ppermute | solution.py:15
  79.2 33.2 %collective-permute-start.8 = (bf16[128,2048]{1,0:T(8,128)(2,1)S(1)}, bf16[128,2048]{1,0:T(8,128)(2,1)S(1)}, u32[]{:S(2)}, u32[]{:S(2)}) collective-permute-start(bf16[128,2048]{1,0:T(8,128)(2,1)S(1)} %bitcast.27), channel_id=1, source_target_pairs={{0,8},{8,0},{1,9},{9,1},{2,10},{10,2},{3,11},{11,3},{4,12},{12,4},... | collective-permute-start | bytes 1572872 | tf_op jit(solution)/shard_map/ppermute | solution.py:19
  83.9 26.4 %collective-permute-start.3 = (bf16[4,128,256]{2,1,0:T(8,128)(2,1)S(1)}, bf16[4,128,256]{2,1,0:T(8,128)(2,1)S(1)}, u32[]{:S(2)}, u32[]{:S(2)}) collective-permute-start(bf16[4,128,256]{2,1,0:T(8,128)(2,1)S(1)} %get-tuple-element.7), channel_id=1, source_target_pairs={{0,2},{1,3},{2,4},{3,5},{4,6},{5,7},{6,0},{7,1},{8,10},{9,11},{10,... | collective-permute-start | bytes 786440 | tf_op jit(solution)/shard_map/ppermute | solution.py:15
  90.3 20.0 %collective-permute-start.4 = (bf16[4,128,256]{2,1,0:T(8,128)(2,1)S(1)}, bf16[4,128,256]{2,1,0:T(8,128)(2,1)S(1)}, u32[]{:S(2)}, u32[]{:S(2)}) collective-permute-start(bf16[4,128,256]{2,1,0:T(8,128)(2,1)S(1)} %get-tuple-element.6), channel_id=1, source_target_pairs={{0,6},{1,7},{2,0},{3,1},{4,2},{5,3},{6,4},{7,5},{8,14},{9,15},{10,... | collective-permute-start | bytes 786440 | tf_op jit(solution)/shard_map/ppermute | solution.py:15
  92.2 18.1 %collective-permute-start.5 = (bf16[2,128,256]{2,1,0:T(8,128)(2,1)S(1)}, bf16[2,128,256]{2,1,0:T(8,128)(2,1)S(1)}, u32[]{:S(2)}, u32[]{:S(2)}) collective-permute-start(bf16[2,128,256]{2,1,0:T(8,128)(2,1)S(1)} %pad_maximum_fusion.11.refs_0_), channel_id=1, source_target_pairs={{0,4},{1,5},{2,6},{3,7},{4,0},{5,1},{6,2},{7,3},{8,12},{9,13},{10,... | collective-permute-start | bytes 393224 | tf_op jit(solution)/shard_map/ppermute | solution.py:15
  110.4 40.6 %collective-permute-start.6 = (bf16[16,128,256]{2,1,0:T(8,128)(2,1)S(1)}, bf16[16,128,256]{2,1,0:T(8,128)(2,1)}, u32[]{:S(2)}, u32[]{:S(2)}) collective-permute-start(bf16[16,128,256]{2,1,0:T(8,128)(2,1)S(1)} %join.1), channel_id=1, source_target_pairs={{0,128},{128,0},{1,129},{129,1},{2,130},{130,2},{3,131},{131,3},{4... | collective-permute-start | bytes 3145736 | tf_op jit(solution)/shard_map/ppermute | solution.py:19
  117.6 26.4 %all-to-all-start.4 = ((bf16[8,32,1024]{2,1,0:T(8,128)(2,1)}), bf16[8,32,1024]{2,1,0:T(8,128)(2,1)S(1)}, u32[]{:S(2)}, u32[]{:S(2)}) async-start(bf16[8,32,1024]{2,1,0:T(8,128)(2,1)} %bitcast.12), calls=%async_computation.4 | async-start | bytes 1048576 | tf_op jit(solution)/shard_map/all_to_all | solution.py:23
  122.8 15.9 %collective-permute-start.7 = (bf16[128,2048]{1,0:T(8,128)(2,1)S(1)}, bf16[128,2048]{1,0:T(8,128)(2,1)S(1)}, u32[]{:S(2)}, u32[]{:S(2)}) collective-permute-start(bf16[128,2048]{1,0:T(8,128)(2,1)S(1)} %bitcast.29), channel_id=1, source_target_pairs={{0,8},{8,0},{1,9},{9,1},{2,10},{10,2},{3,11},{11,3},{4,12},{12,4},... | collective-permute-start | bytes 1572872 | tf_op jit(solution)/shard_map/ppermute | solution.py:19
  144.0 23.7 %all-to-all-start.2 = ((bf16[8,32,1024]{2,1,0:T(8,128)(2,1)}), bf16[8,32,1024]{2,1,0:T(8,128)(2,1)S(1)}, u32[]{:S(2)}, u32[]{:S(2)}) async-start(bf16[8,32,1024]{2,1,0:T(8,128)(2,1)} %bitcast.8), calls=%async_computation.2 | async-start | bytes 1048576 | tf_op jit(solution)/shard_map/all_to_all | solution.py:23

commit v3 on v1

--- a/solution.py
+++ b/solution.py
@@ -6,10 +6,11 @@
 from jax.sharding import Mesh, PartitionSpec as P
 
 VMEM = 20 * 1024 * 1024
+HALF_VMEM = 50 * 1024 * 1024
 AXES = ("hi", "core", "rowpair", "side", "lo", "z")
 
 
-SHIFTS = (3, -3, 2, -2, 1, -1, 4)
+SHIFTS = (3, -3, 2, -2, 4, 1, -1)
 
 
 def shift(x, by):
@@ -50,20 +51,45 @@
     )(*blocks)
 
 
+def half_kernel(weight_ref, out_ref, sem):
+    part = out_ref.shape[0]
+    rows = pl.ds(pl.multiple_of(lax.axis_index("core") * part, part), part)
+    copy = pltpu.make_async_copy(weight_ref.at[rows], out_ref, sem)
+    copy.start()
+    copy.wait()
+
+
+def half_of(weight, part):
+    shape = (part, weight.shape[1])
+    return pl.pallas_call(
+        half_kernel,
+        in_specs=[pl.BlockSpec(memory_space=pl.ANY)],
+        out_specs=pl.BlockSpec(memory_space=pltpu.VMEM),
+        out_shape=jax.ShapeDtypeStruct(shape, weight.dtype),
+        scratch_shapes=[pltpu.SemaphoreType.DMA],
+        cost_estimate=pl.CostEstimate(flops=0, bytes_accessed=2 * weight.size, transcendentals=0),
+        compiler_params=pltpu.CompilerParams(vmem_limit_bytes=HALF_VMEM),
+        name="half",
+    )(weight)
+
+
 def product_kernel(near_ref, far_ref, weight_ref, near_other_ref, last_other_ref, out_ref, own_ref, sems):
     core, low = lax.axis_index("core"), lax.axis_index("lo")
     count = near_ref.shape[0]
     part, inner = near_other_ref.shape
     halves = [pl.ds(pl.multiple_of(at * part, part), part) for at in (core, 1 - core)]
-    copies = [pltpu.make_async_copy(weight_ref.at[rows], own_ref.at[i], sems.at[i]) for i, rows in enumerate(halves)]
-    for copy in copies:
+    sources = [weight_ref.at[rows] for rows in halves] + [near_other_ref]
+    copies = [pltpu.make_async_copy(source, own_ref.at[i], sems.at[i]) for i, source in enumerate(sources)]
+    for copy in reversed(copies):
         copy.start()
 
     def term(weight, at):
         panel = jnp.concatenate([near_ref[:, at : at + inner], far_ref[:, at : at + inner]], axis=0)
         return lax.dot_general(weight, panel, (((1,), (1,)), ((), ())), preferred_element_type=jnp.float32)
 
-    others = [term(ref[...], inner) for ref in (near_other_ref, last_other_ref)]
+    last = term(last_other_ref[...], inner)
+    copies[2].wait()
+    others = [term(own_ref[2], inner), last]
     for i, rows in enumerate(halves):
         copies[i].wait()
         sums = (term(own_ref[i], 0) + others[i]).T.astype(out_ref.dtype)
@@ -76,10 +102,10 @@
     flops = 4 * near.size * outs
     return pl.pallas_call(
         product_kernel,
-        in_specs=[pl.BlockSpec(memory_space=pl.ANY if i == 2 else pltpu.VMEM) for i in range(5)],
+        in_specs=[pl.BlockSpec(memory_space=pl.ANY if i in (2, 3) else pltpu.VMEM) for i in range(5)],
         out_specs=pl.BlockSpec(memory_space=pltpu.VMEM),
         out_shape=jax.ShapeDtypeStruct((2 * count, outs), jnp.bfloat16),
-        scratch_shapes=[pltpu.VMEM((2, outs // 2, near.shape[1] // 2), jnp.bfloat16), pltpu.SemaphoreType.DMA((2,))],
+        scratch_shapes=[pltpu.VMEM((3, outs // 2, near.shape[1] // 2), jnp.bfloat16), pltpu.SemaphoreType.DMA((3,))],
         cost_estimate=pl.CostEstimate(flops=flops, bytes_accessed=8 * outs * near.shape[1], transcendentals=0),
         compiler_params=pltpu.CompilerParams(vmem_limit_bytes=44 * 1024 * 1024),
         name="products",
@@ -109,7 +135,7 @@
     arrived = exchange(tiles, ("hi", "core", "rowpair", "side"))
 
     part = outs // 2
-    near_weight = lax.dynamic_slice_in_dim(cycle_weight, core * part, part, axis=0)
+    near_weight = half_of(cycle_weight, part)
     near_other = swap(near_weight, "side")
     last_other = swap(near_other, "core")
 

time: 173 us -> 170 us (0.983)
  local copies, waits for them, and re-layouts: 7.35 us -> 4.13 us
  waiting for transfers between devices: 70.1 us -> 67.2 us
  Pallas kernels: 8.3 us -> 10.5 us
    ppermute x7, waiting for transfers between devices: 17.2 us -> 12.7 us  [shift(): return lax.ppermute(x, 'z', [(i, (i + by) % depth) for i in range(depth)])]
    dynamic_slice x1 -> x0, local copies, waits for them, and re-layouts: 3.22 us -> none  [body(): lax.dynamic_slice_in_dim(cycle_weight, core * part, part, axis=0)]
  transfers between devices with their start and end apart: 15 -> 15, of which waited for: 7 -> 8; matrix products, arithmetic and copies ran while one was open for 4% -> 4% of each run, Pallas kernels for 5% -> 5%
where the time goes in v3:
time: 170 us; the launch traced here: 169 us
  starting transfers between devices  81.9 us (48%)
  waiting for transfers between devices  67.2 us (40%)
  Pallas kernels  10.5 us (6%)
  local copies, waits for them, and re-layouts  4.13 us (2%)
  matrix products  3.76 us (2%)
    all_to_all x3, waiting for transfers between devices, exchange(): return lax.all_to_all(x, axes, 0, 0, tiled=True)  52.2 us
    all_to_all x3, starting transfers between devices, exchange(): return lax.all_to_all(x, axes, 0, 0, tiled=True)  35.9 us
    ppermute x7, starting transfers between devices, shift(): return lax.ppermute(x, 'z', [(i, (i + by) % depth) for i in range(depth)])  24 us
    ppermute x5, starting transfers between devices, swap(): return lax.ppermute(x, axis, [(0, 1), (1, 0)])  22 us
    ppermute x7, waiting for transfers between devices, shift(): return lax.ppermute(x, 'z', [(i, (i + by) % depth) for i in range(depth)])  12.7 us
    pallas_call x1, Pallas kernels, products(): pl.pallas_call(product_kernel, in_specs=[pl.BlockSpec(memory_space=pl.ANY...  6.8 us
    dot_general x1, matrix products, body(): jnp.einsum('pad,pbd->ab', dressed, whole, preferred_element_type=jnp.floa...  3.54 us
  transfers between devices with their start and end apart: 15, of which 8 were waited for; matrix products, arithmetic and copies ran while one was open for 4% of the time, Pallas kernels for 5%

profile of v3, /device:TPU:1, one launch (start us, length us, event | category | flops | bytes accessed | tf_op | source)
XLA Modules:
  0.0 169.4 jit_solution(12549397292532818766)
XLA Ops:
  0.7 1.7 half.1
  2.3 4.1 %collective-permute-start.10 = (bf16[512,2048]{1,0:T(8,128)(2,1)S(1)}, bf16[512,2048]{1,0:T(8,128)(2,1)}, u32[]{:S(2)}, u32[]{:S(2)}) collective-permute-start(bf16[512,2048]{1,0:T(8,128)(2,1)S(1)} %half.1), channel_id=1, source_target_pairs={{0,16},{16,0},{1,17},{17,1},{2,18},{18,2},{3,19},{19,3},{4,20},{20... | collective-permute-start | bytes 6291464 | tf_op jit(solution)/shard_map/ppermute | solution.py:22
  6.9 0.8 reshape.46
  7.7 16.0 %all-to-all-start = ((bf16[64,8,128]{2,1,0:T(8,128)(2,1)}), bf16[64,8,128]{2,1,0:T(8,128)(2,1)S(1)}, u32[]{:S(2)}, u32[]{:S(2)}) async-start(bf16[64,8,128]{2,1,0:T(8,128)(2,1)} %reshape.46), calls=%async_computation | async-start | bytes 262144 | tf_op jit(solution)/shard_map/all_to_all | solution.py:30
  23.8 36.6 %all-to-all-done = bf16[64,8,128]{2,1,0:T(8,128)(2,1)S(1)} async-done(((bf16[64,8,128]{2,1,0:T(8,128)(2,1)}), bf16[64,8,128]{2,1,0:T(8,128)(2,1)S(1)}, u32[]{:S(2)}, u32[]{:S(2)}) %all-to-all-start) | async-done | bytes 131104 | tf_op jit(solution)/shard_map/all_to_all | solution.py:30
  61.0 1.1 broadcast_in_dim.2
  62.0 16.4 %all-to-all-start.1 = ((bf16[8,16,4096]{2,1,0:T(8,128)(2,1)}), bf16[8,16,4096]{2,1,0:T(8,128)(2,1)S(1)}, u32[]{:S(2)}, u32[]{:S(2)}) async-start(bf16[8,16,4096]{2,1,0:T(8,128)(2,1)} %broadcast_in_dim.2), calls=%async_computation.1 | async-start | bytes 2097152 | tf_op jit(solution)/shard_map/all_to_all | solution.py:30
  78.4 2.6 %collective-permute-start.11 = (bf16[512,2048]{1,0:T(8,128)(2,1)}, bf16[512,2048]{1,0:T(8,128)(2,1)S(1)}, u32[]{:S(2)}, u32[]{:S(2)}) collective-permute-start(bf16[512,2048]{1,0:T(8,128)(2,1)} %collective-permute-done.10.near_other_ref), channel_id=1, source_target_pairs={{0,128},{128,0},{1,129},{129,1},{2,130},{130,2},{3,131},{131,3},{4... | collective-permute-start | bytes 6291464 | tf_op jit(solution)/shard_map/ppermute | solution.py:22
  81.1 3.1 %collective-permute-start = (bf16[1,128,256]{2,1,0:T(8,128)(2,1)S(1)}, bf16[1,128,256]{2,1,0:T(8,128)(2,1)S(1)}, u32[]{:S(2)}, u32[]{:S(2)}) collective-permute-start(bf16[1,128,256]{2,1,0:T(8,128)(2,1)S(1)} %constant_dynamic-slice_fusion), channel_id=1, source_target_pairs={{0,8},{8,0},{1,9},{9,1},{2,10},{10,2},{3,11},{11,3},{4,12},{12,4},... | collective-permute-start | bytes 196616 | tf_op jit(solution)/shard_map/ppermute | solution.py:22
  84.2 2.4 %collective-permute-done = bf16[1,128,256]{2,1,0:T(8,128)(2,1)S(1)} collective-permute-done((bf16[1,128,256]{2,1,0:T(8,128)(2,1)S(1)}, bf16[1,128,256]{2,1,0:T(8,128)(2,1)S(1)}, u32[]{:S(2)}, u32[]{:S(2)}) %collective-permute-start) | collective-permute-done | bytes 65568 | tf_op jit(solution)/shard_map/ppermute | solution.py:22
  86.6 4.8 %collective-permute-start.7 = (bf16[2,128,256]{2,1,0:T(8,128)(2,1)S(1)}, bf16[2,128,256]{2,1,0:T(8,128)(2,1)S(1)}, u32[]{:S(2)}, u32[]{:S(2)}) collective-permute-start(bf16[2,128,256]{2,1,0:T(8,128)(2,1)S(1)} %pad_maximum_fusion.8.refs_0_), channel_id=1, source_target_pairs={{0,7},{1,0},{2,1},{3,2},{4,3},{5,4},{6,5},{7,6},{8,15},{9,8},{10,9... | collective-permute-start | bytes 393224 | tf_op jit(solution)/shard_map/ppermute | solution.py:18
  91.5 1.9 %collective-permute-start.6 = (bf16[2,128,256]{2,1,0:T(8,128)(2,1)S(1)}, bf16[2,128,256]{2,1,0:T(8,128)(2,1)}, u32[]{:S(2)}, u32[]{:S(2)}) collective-permute-start(bf16[2,128,256]{2,1,0:T(8,128)(2,1)S(1)} %pad_maximum_fusion.8.refs_0_), channel_id=1, source_target_pairs={{0,1},{1,2},{2,3},{3,4},{4,5},{5,6},{6,7},{7,0},{8,9},{9,10},{10,1... | collective-permute-start | bytes 393224 | tf_op jit(solution)/shard_map/ppermute | solution.py:18
  93.4 6.1 %collective-permute-start.5 = (bf16[2,128,256]{2,1,0:T(8,128)(2,1)S(1)}, bf16[2,128,256]{2,1,0:T(8,128)(2,1)}, u32[]{:S(2)}, u32[]{:S(2)}) collective-permute-start(bf16[2,128,256]{2,1,0:T(8,128)(2,1)S(1)} %pad_maximum_fusion.8.refs_0_), channel_id=1, source_target_pairs={{0,4},{1,5},{2,6},{3,7},{4,0},{5,1},{6,2},{7,3},{8,12},{9,13},{10,... | collective-permute-start | bytes 393224 | tf_op jit(solution)/shard_map/ppermute | solution.py:18
  99.5 2.2 %collective-permute-start.4 = (bf16[2,128,256]{2,1,0:T(8,128)(2,1)S(1)}, bf16[2,128,256]{2,1,0:T(8,128)(2,1)}, u32[]{:S(2)}, u32[]{:S(2)}) collective-permute-start(bf16[2,128,256]{2,1,0:T(8,128)(2,1)S(1)} %pad_maximum_fusion.8.refs_0_), channel_id=1, source_target_pairs={{0,6},{1,7},{2,0},{3,1},{4,2},{5,3},{6,4},{7,5},{8,14},{9,15},{10,... | collective-permute-start | bytes 393224 | tf_op jit(solution)/shard_map/ppermute | solution.py:18
  101.7 4.1 %collective-permute-done.7.refs_7_ = bf16[2,128,256]{2,1,0:T(8,128)(2,1)S(1)} collective-permute-done((bf16[2,128,256]{2,1,0:T(8,128)(2,1)S(1)}, bf16[2,128,256]{2,1,0:T(8,128)(2,1)S(1)}, u32[]{:S(2)}, u32[]{:S(2)}) %collective-permute-start.7) | collective-permute-done | bytes 131104 | tf_op jit(solution)/shard_map/ppermute | solution.py:18
  105.8 1.9 %all-to-all-done.1 = bf16[8,16,4096]{2,1,0:T(8,128)(2,1)S(1)} async-done(((bf16[8,16,4096]{2,1,0:T(8,128)(2,1)}), bf16[8,16,4096]{2,1,0:T(8,128)(2,1)S(1)}, u32[]{:S(2)}, u32[]{:S(2)}) %all-to-all-start.1) | async-done | bytes 1048608 | tf_op jit(solution)/shard_map/all_to_all | solution.py:30
  107.7 3.1 %collective-permute-start.9 = (bf16[8,16,4096]{2,1,0:T(8,128)(2,1)S(1)}, bf16[8,16,4096]{2,1,0:T(8,128)(2,1)}, u32[]{:S(2)}, u32[]{:S(2)}) collective-permute-start(bf16[8,16,4096]{2,1,0:T(8,128)(2,1)S(1)} %all-to-all-done.1), channel_id=1, source_target_pairs={{0,8},{8,0},{1,9},{9,1},{2,10},{10,2},{3,11},{11,3},{4,12},{12,4},... | collective-permute-start | bytes 3145736 | tf_op jit(solution)/shard_map/ppermute | solution.py:22
  110.8 1.9 %collective-permute-start.3 = (bf16[2,128,256]{2,1,0:T(8,128)(2,1)S(1)}, bf16[2,128,256]{2,1,0:T(8,128)(2,1)S(1)}, u32[]{:S(2)}, u32[]{:S(2)}) collective-permute-start(bf16[2,128,256]{2,1,0:T(8,128)(2,1)S(1)} %pad_maximum_fusion.8.refs_0_), channel_id=1, source_target_pairs={{0,2},{1,3},{2,4},{3,5},{4,6},{5,7},{6,0},{7,1},{8,10},{9,11},{10,... | collective-permute-start | bytes 393224 | tf_op jit(solution)/shard_map/ppermute | solution.py:18
  112.8 3.5 %collective-permute-done.5.refs_5_ = bf16[2,128,256]{2,1,0:T(8,128)(2,1)} collective-permute-done((bf16[2,128,256]{2,1,0:T(8,128)(2,1)S(1)}, bf16[2,128,256]{2,1,0:T(8,128)(2,1)}, u32[]{:S(2)}, u32[]{:S(2)}) %collective-permute-start.5) | collective-permute-done | bytes 131104 | tf_op jit(solution)/shard_map/ppermute | solution.py:18
  116.2 1.9 %collective-permute-start.2 = (bf16[2,128,256]{2,1,0:T(8,128)(2,1)S(1)}, bf16[2,128,256]{2,1,0:T(8,128)(2,1)S(1)}, u32[]{:S(2)}, u32[]{:S(2)}) collective-permute-start(bf16[2,128,256]{2,1,0:T(8,128)(2,1)S(1)} %pad_maximum_fusion.8.refs_0_), channel_id=1, source_target_pairs={{0,5},{1,6},{2,7},{3,0},{4,1},{5,2},{6,3},{7,4},{8,13},{9,14},{10,... | collective-permute-start | bytes 393224 | tf_op jit(solution)/shard_map/ppermute | solution.py:18
  118.2 5.2 %collective-permute-start.1 = (bf16[2,128,256]{2,1,0:T(8,128)(2,1)S(1)}, bf16[2,128,256]{2,1,0:T(8,128)(2,1)S(1)}, u32[]{:S(2)}, u32[]{:S(2)}) collective-permute-start(bf16[2,128,256]{2,1,0:T(8,128)(2,1)S(1)} %pad_maximum_fusion.8.refs_0_), channel_id=1, source_target_pairs={{0,3},{1,4},{2,5},{3,6},{4,7},{5,0},{6,1},{7,2},{8,11},{9,12},{10,... | collective-permute-start | bytes 393224 | tf_op jit(solution)/shard_map/ppermute | solution.py:18
  123.4 4.3 %collective-permute-done.2.refs_2_ = bf16[2,128,256]{2,1,0:T(8,128)(2,1)S(1)} collective-permute-done((bf16[2,128,256]{2,1,0:T(8,128)(2,1)S(1)}, bf16[2,128,256]{2,1,0:T(8,128)(2,1)S(1)}, u32[]{:S(2)}, u32[]{:S(2)}) %collective-permute-start.2) | collective-permute-done | bytes 131104 | tf_op jit(solution)/shard_map/ppermute | solution.py:18
  127.7 0.7 collective-permute-done.1.refs_1_
  128.4 2.1 %join.1 = bf16[16,128,256]{2,1,0:T(8,128)(2,1)} custom-call(bf16[2,128,256]{2,1,0:T(8,128)(2,1)S(1)} %pad_maximum_fusion.8.refs_0_, bf16[2,128,256]{2,1,0:T(8,128)(2,1)S(1)} %collective-permute-done.1.refs_1_, bf16[2,128,256]{2,1,0:T(8,128)(2,1)S(1)} %collective-permute-done.2.refs_2_, bf16[2,128,256]{2,1,0:T(8,128)(2,1)S(1)} %collective-permute-done.3.refs_3_, ...), custom_call_target="tpu_custom_call" | custom-call | bytes 2097152 | tf_op jit(solution)/shard_map/join/pallas_call | solution.py:43
  130.5 9.1 %collective-permute-start.8 = (bf16[16,128,256]{2,1,0:T(8,128)(2,1)}, bf16[16,128,256]{2,1,0:T(8,128)(2,1)}, u32[]{:S(2)}, u32[]{:S(2)}) collective-permute-start(bf16[16,128,256]{2,1,0:T(8,128)(2,1)} %join.1), channel_id=1, source_target_pairs={{0,128},{128,0},{1,129},{129,1},{2,130},{130,2},{3,131},{131,3},{4... | collective-permute-start | bytes 3145736 | tf_op jit(solution)/shard_map/ppermute | solution.py:22
  139.6 6.8 %products.1 = bf16[256,1024]{1,0:T(8,128)(2,1)S(1)} custom-call(bf16[128,4096]{1,0:T(8,128)(2,1)S(1)} %bitcast.34, bf16[128,4096]{1,0:T(8,128)(2,1)} %bitcast.9.far_ref, bf16[1024,2048]{1,0:T(8,128)(2,1)} %weight_ref.3, bf16[512,2048]{1,0:T(8,128)(2,1)} %collective-permute-done.10.near_other_ref, bf16[512,2048]{1,0:T(8,128)(2,1)S(1)} %collective-permute-done.11.last_other_ref), custom_call_target="tpu_custom_call" | custom-call | flops 2147483648 | bytes 33554432 | tf_op jit(solution)/shard_map/products/pallas_call | solution.py:103
  146.4 0.8 copy-done.1
  147.2 3.5 %all-to-all-start.2 = ((bf16[8,32,1024]{2,1,0:T(8,128)(2,1)}), bf16[8,32,1024]{2,1,0:T(8,128)(2,1)S(1)}, u32[]{:S(2)}, u32[]{:S(2)}) async-start(bf16[8,32,1024]{2,1,0:T(8,128)(2,1)} %bitcast.35), calls=%async_computation.2 | async-start | bytes 1048576 | tf_op jit(solution)/shard_map/all_to_all | solution.py:30
  150.7 3.5 %fusion.4 = bf16[256,256]{1,0:T(8,128)(2,1)S(1)} fusion(bf16[16,128,256]{2,1,0:T(8,128)(2,1)} %collective-permute-done.8, bf16[16,128,256]{2,1,0:T(8,128)(2,1)} %join.1, bf16[1,1,256,256]{3,2,1,0:T(8,128)(2,1)S(1)} %copy-done), kind=kOutput, calls=%fused_computation.4 | convolution fusion | flops 1083179008 | bytes 2359296 | tf_op jit(solution)/shard_map/pad,pbd->ab/dot_general | solution.py:159
  154.3 0.7 fusion.11
  155.0 13.7 %all-to-all-done.2 = bf16[8,32,1024]{2,1,0:T(8,128)(2,1)S(1)} async-done(((bf16[8,32,1024]{2,1,0:T(8,128)(2,1)}), bf16[8,32,1024]{2,1,0:T(8,128)(2,1)S(1)}, u32[]{:S(2)}, u32[]{:S(2)}) %all-to-all-start.2) | async-done | bytes 524320 | tf_op jit(solution)/shard_map/all_to_all | solution.py:30
  168.7 0.7 copy.12
  (27 shorter events, 1.2 us)
Async XLA Ops:
  0.6 5.8 %copy-start = (bf16[1,1,256,256]{3,2,1,0:T(8,128)(2,1)S(1)}, bf16[1,1,256,256]{3,2,1,0:T(8,128)(2,1)}, u32[]{:S(2)}) copy-start(bf16[1,1,256,256]{3,2,1,0:T(8,128)(2,1)} %param.4) | copy-start | bytes 393220
  0.6 5.8 %copy-start.3 = (s32[256]{0:T(256)S(1)}, s32[256]{0:T(256)}, u32[]{:S(2)}) copy-start(s32[256]{0:T(256)} %param.7) | copy-start | bytes 3076
  2.3 76.1 %collective-permute-start.10 = (bf16[512,2048]{1,0:T(8,128)(2,1)S(1)}, bf16[512,2048]{1,0:T(8,128)(2,1)}, u32[]{:S(2)}, u32[]{:S(2)}) collective-permute-start(bf16[512,2048]{1,0:T(8,128)(2,1)S(1)} %half.1), channel_id=1, source_target_pairs={{0,16},{16,0},{1,17},{17,1},{2,18},{18,2},{3,19},{19,3},{4,20},{20... | collective-permute-start | bytes 6291464 | tf_op jit(solution)/shard_map/ppermute | solution.py:22
  7.7 52.6 %all-to-all-start = ((bf16[64,8,128]{2,1,0:T(8,128)(2,1)}), bf16[64,8,128]{2,1,0:T(8,128)(2,1)S(1)}, u32[]{:S(2)}, u32[]{:S(2)}) async-start(bf16[64,8,128]{2,1,0:T(8,128)(2,1)} %reshape.46), calls=%async_computation | async-start | bytes 262144 | tf_op jit(solution)/shard_map/all_to_all | solution.py:30
  60.6 20.5 %copy-start.2 = (bf16[1,256,256]{2,1,0:T(8,128)(2,1)S(1)}, bf16[1,256,256]{2,1,0:T(8,128)(2,1)}, u32[]{:S(2)}) copy-start(bf16[1,256,256]{2,1,0:T(8,128)(2,1)} %param.5) | copy-start | bytes 393220
  62.0 45.7 %all-to-all-start.1 = ((bf16[8,16,4096]{2,1,0:T(8,128)(2,1)}), bf16[8,16,4096]{2,1,0:T(8,128)(2,1)S(1)}, u32[]{:S(2)}, u32[]{:S(2)}) async-start(bf16[8,16,4096]{2,1,0:T(8,128)(2,1)} %broadcast_in_dim.2), calls=%async_computation.1 | async-start | bytes 2097152 | tf_op jit(solution)/shard_map/all_to_all | solution.py:30
  78.4 61.1 %collective-permute-start.11 = (bf16[512,2048]{1,0:T(8,128)(2,1)}, bf16[512,2048]{1,0:T(8,128)(2,1)S(1)}, u32[]{:S(2)}, u32[]{:S(2)}) collective-permute-start(bf16[512,2048]{1,0:T(8,128)(2,1)} %collective-permute-done.10.near_other_ref), channel_id=1, source_target_pairs={{0,128},{128,0},{1,129},{129,1},{2,130},{130,2},{3,131},{131,3},{4... | collective-permute-start | bytes 6291464 | tf_op jit(solution)/shard_map/ppermute | solution.py:22
  81.1 5.5 %collective-permute-start = (bf16[1,128,256]{2,1,0:T(8,128)(2,1)S(1)}, bf16[1,128,256]{2,1,0:T(8,128)(2,1)S(1)}, u32[]{:S(2)}, u32[]{:S(2)}) collective-permute-start(bf16[1,128,256]{2,1,0:T(8,128)(2,1)S(1)} %constant_dynamic-slice_fusion), channel_id=1, source_target_pairs={{0,8},{8,0},{1,9},{9,1},{2,10},{10,2},{3,11},{11,3},{4,12},{12,4},... | collective-permute-start | bytes 196616 | tf_op jit(solution)/shard_map/ppermute | solution.py:22
  86.6 19.2 %collective-permute-start.7 = (bf16[2,128,256]{2,1,0:T(8,128)(2,1)S(1)}, bf16[2,128,256]{2,1,0:T(8,128)(2,1)S(1)}, u32[]{:S(2)}, u32[]{:S(2)}) collective-permute-start(bf16[2,128,256]{2,1,0:T(8,128)(2,1)S(1)} %pad_maximum_fusion.8.refs_0_), channel_id=1, source_target_pairs={{0,7},{1,0},{2,1},{3,2},{4,3},{5,4},{6,5},{7,6},{8,15},{9,8},{10,9... | collective-permute-start | bytes 393224 | tf_op jit(solution)/shard_map/ppermute | solution.py:18
  91.5 19.4 %collective-permute-start.6 = (bf16[2,128,256]{2,1,0:T(8,128)(2,1)S(1)}, bf16[2,128,256]{2,1,0:T(8,128)(2,1)}, u32[]{:S(2)}, u32[]{:S(2)}) collective-permute-start(bf16[2,128,256]{2,1,0:T(8,128)(2,1)S(1)} %pad_maximum_fusion.8.refs_0_), channel_id=1, source_target_pairs={{0,1},{1,2},{2,3},{3,4},{4,5},{5,6},{6,7},{7,0},{8,9},{9,10},{10,1... | collective-permute-start | bytes 393224 | tf_op jit(solution)/shard_map/ppermute | solution.py:18
  93.4 22.8 %collective-permute-start.5 = (bf16[2,128,256]{2,1,0:T(8,128)(2,1)S(1)}, bf16[2,128,256]{2,1,0:T(8,128)(2,1)}, u32[]{:S(2)}, u32[]{:S(2)}) collective-permute-start(bf16[2,128,256]{2,1,0:T(8,128)(2,1)S(1)} %pad_maximum_fusion.8.refs_0_), channel_id=1, source_target_pairs={{0,4},{1,5},{2,6},{3,7},{4,0},{5,1},{6,2},{7,3},{8,12},{9,13},{10,... | collective-permute-start | bytes 393224 | tf_op jit(solution)/shard_map/ppermute | solution.py:18
  99.5 18.7 %collective-permute-start.4 = (bf16[2,128,256]{2,1,0:T(8,128)(2,1)S(1)}, bf16[2,128,256]{2,1,0:T(8,128)(2,1)}, u32[]{:S(2)}, u32[]{:S(2)}) collective-permute-start(bf16[2,128,256]{2,1,0:T(8,128)(2,1)S(1)} %pad_maximum_fusion.8.refs_0_), channel_id=1, source_target_pairs={{0,6},{1,7},{2,0},{3,1},{4,2},{5,3},{6,4},{7,5},{8,14},{9,15},{10,... | collective-permute-start | bytes 393224 | tf_op jit(solution)/shard_map/ppermute | solution.py:18
  107.7 31.9 %collective-permute-start.9 = (bf16[8,16,4096]{2,1,0:T(8,128)(2,1)S(1)}, bf16[8,16,4096]{2,1,0:T(8,128)(2,1)}, u32[]{:S(2)}, u32[]{:S(2)}) collective-permute-start(bf16[8,16,4096]{2,1,0:T(8,128)(2,1)S(1)} %all-to-all-done.1), channel_id=1, source_target_pairs={{0,8},{8,0},{1,9},{9,1},{2,10},{10,2},{3,11},{11,3},{4,12},{12,4},... | collective-permute-start | bytes 3145736 | tf_op jit(solution)/shard_map/ppermute | solution.py:22
  110.8 12.5 %collective-permute-start.3 = (bf16[2,128,256]{2,1,0:T(8,128)(2,1)S(1)}, bf16[2,128,256]{2,1,0:T(8,128)(2,1)S(1)}, u32[]{:S(2)}, u32[]{:S(2)}) collective-permute-start(bf16[2,128,256]{2,1,0:T(8,128)(2,1)S(1)} %pad_maximum_fusion.8.refs_0_), channel_id=1, source_target_pairs={{0,2},{1,3},{2,4},{3,5},{4,6},{5,7},{6,0},{7,1},{8,10},{9,11},{10,... | collective-permute-start | bytes 393224 | tf_op jit(solution)/shard_map/ppermute | solution.py:18
  116.2 11.4 %collective-permute-start.2 = (bf16[2,128,256]{2,1,0:T(8,128)(2,1)S(1)}, bf16[2,128,256]{2,1,0:T(8,128)(2,1)S(1)}, u32[]{:S(2)}, u32[]{:S(2)}) collective-permute-start(bf16[2,128,256]{2,1,0:T(8,128)(2,1)S(1)} %pad_maximum_fusion.8.refs_0_), channel_id=1, source_target_pairs={{0,5},{1,6},{2,7},{3,0},{4,1},{5,2},{6,3},{7,4},{8,13},{9,14},{10,... | collective-permute-start | bytes 393224 | tf_op jit(solution)/shard_map/ppermute | solution.py:18
  118.2 10.2 %collective-permute-start.1 = (bf16[2,128,256]{2,1,0:T(8,128)(2,1)S(1)}, bf16[2,128,256]{2,1,0:T(8,128)(2,1)S(1)}, u32[]{:S(2)}, u32[]{:S(2)}) collective-permute-start(bf16[2,128,256]{2,1,0:T(8,128)(2,1)S(1)} %pad_maximum_fusion.8.refs_0_), channel_id=1, source_target_pairs={{0,3},{1,4},{2,5},{3,6},{4,7},{5,0},{6,1},{7,2},{8,11},{9,12},{10,... | collective-permute-start | bytes 393224 | tf_op jit(solution)/shard_map/ppermute | solution.py:18
  130.5 20.2 %collective-permute-start.8 = (bf16[16,128,256]{2,1,0:T(8,128)(2,1)}, bf16[16,128,256]{2,1,0:T(8,128)(2,1)}, u32[]{:S(2)}, u32[]{:S(2)}) collective-permute-start(bf16[16,128,256]{2,1,0:T(8,128)(2,1)} %join.1), channel_id=1, source_target_pairs={{0,128},{128,0},{1,129},{129,1},{2,130},{130,2},{3,131},{131,3},{4... | collective-permute-start | bytes 3145736 | tf_op jit(solution)/shard_map/ppermute | solution.py:22
  146.4 0.8 copy-start.1
  147.2 21.5 %all-to-all-start.2 = ((bf16[8,32,1024]{2,1,0:T(8,128)(2,1)}), bf16[8,32,1024]{2,1,0:T(8,128)(2,1)S(1)}, u32[]{:S(2)}, u32[]{:S(2)}) async-start(bf16[8,32,1024]{2,1,0:T(8,128)(2,1)} %bitcast.35), calls=%async_computation.2 | async-start | bytes 1048576 | tf_op jit(solution)/shard_map/all_to_all | solution.py:30
